TPU v7x, 32 devices: a whole 2x2x4 slice. The times are simulated.
32 devices in a mesh: depth: 16 (over z, x, core), gx: 2 (over y).
Axes of the slice: x: 2, y: 2, z: 4, core: 2. Of those that a mesh axis runs over, the one named last changes fastest.
Arguments:
- density: float32 [32, 16, 1024], P('depth', 'gx'), may hold values from 0.25 to 2
- tf_index: int32 [32, 16, 1024], P('depth', 'gx'), may hold values from 0 to 255
- tf_table: float32 [4, 256], replicated, may hold values from 0.3 to 3
Outputs:
- image: float32 [4, 16, 1024], P(None, 'gx', 'depth')
All inputs are finite; a program needn't handle non-finite values.
Results may differ from a plain program's by a relative error of at most 0.00011.
Values sent between devices are 32-bit elements; how exact they have to be, the bound alone decides.
No kernel may reach another device: no remote copies, remote signals or barrier semaphores. Data moves between devices by JAX's collectives and lax.ppermute only.
A program may use at most 64 MiB of HBM per device.

v0:
```python
import jax
import jax.numpy as jnp
from jax import lax
from jax.sharding import PartitionSpec as P


def extended(cells, sides, width):
    for axis, dim in sides:
        count = lax.axis_size(axis)
        ends = count - 1
        head = lax.slice_in_dim(cells, 0, width, axis=dim)
        tail = lax.slice_in_dim(cells, cells.shape[dim] - width, cells.shape[dim], axis=dim)
        cells = jnp.concatenate(
            [
                lax.ppermute(tail, axis, [(i, (i + 1) % count) for i in range(ends)]),
                cells,
                lax.ppermute(head, axis, [((i + 1) % count, i) for i in range(ends)]),
            ],
            axis=dim,
        )
    return cells


def entering(array, axis, combine, identity):
    peers, mine = (lax.axis_size(axis), lax.axis_index(axis))
    everything = lax.all_gather(array, axis)
    start = jnp.broadcast_to(jnp.asarray(identity, array.dtype), array.shape)

    def step(k, before):
        reached = k < mine
        new = combine(before, everything[k])
        return jnp.where(reached, new, before)

    return lax.fori_loop(0, peers, step, start)


def smooth(value, axis):
    size = value.shape[axis]
    return (
        lax.slice_in_dim(value, 0, size - 2, axis=axis)
        + 2.0 * lax.slice_in_dim(value, 1, size - 1, axis=axis)
        + lax.slice_in_dim(value, 2, size, axis=axis)
    )


def differ(value, axis):
    size = value.shape[axis]
    return lax.slice_in_dim(value, 2, size, axis=axis) - lax.slice_in_dim(
        value, 0, size - 2, axis=axis
    )


def shade(grad_z, grad_x, grad_y, dens, entry, step_len):
    inverse = lax.rsqrt(grad_z * grad_z + grad_x * grad_x + grad_y * grad_y + 1.0)
    ndl = (0.48 * grad_z + 0.6 * grad_x + 0.64 * grad_y) * inverse
    ndh = (0.86023 * grad_z + 0.34875 * grad_x + 0.372 * grad_y) * inverse
    shine = jnp.maximum(ndh, 0.0)
    shine = shine * shine
    shine = shine * shine
    shine = shine * shine
    lit = 0.3 + 0.6 * jnp.abs(ndl) + 0.4 * shine
    alpha = 1.0 - jnp.exp(-entry[3] * dens * step_len)
    emit = entry[:3] * (alpha * lit)
    return (emit, 1.0 - alpha)


def front_products(transmit):
    running = jnp.cumprod(transmit, axis=0)
    leading = jnp.ones_like(transmit[:1])
    return (jnp.concatenate([leading, running[:-1]], axis=0), running[-1])


def table_entries(tf_table, tf_index):
    depth_len, width, length = tf_index.shape
    entries_count = tf_table.shape[1]
    rows = tf_index.reshape(depth_len * width, length)
    levels = jnp.arange(entries_count, dtype=jnp.int32)

    def lookup(row):
        onehot = (row[:, None] == levels[None, :]).astype(jnp.float32)
        return lax.dot_general(
            tf_table,
            onehot,
            (((1,), (1,)), ((), ())),
            precision=lax.Precision.HIGHEST,
            preferred_element_type=jnp.float32,
        )

    looked = lax.map(lookup, rows)
    looked = looked.reshape(depth_len, width, 4, length)
    return jnp.transpose(looked, (2, 0, 1, 3))


def body(density, tf_index, tf_table):
    bricks = lax.axis_size("depth")
    step_len = 1.0 / (density.shape[0] * bricks)
    bordered = extended(density, (("depth", 0), ("gx", 1)), 1)
    padded = jnp.pad(bordered, ((0, 0), (0, 0), (1, 1)))
    grad_z = smooth(smooth(differ(padded, 0), 1), 2) / 2.0
    summed = smooth(padded, 0)
    grad_x = smooth(differ(summed, 1), 2) / 2.0
    grad_y = differ(smooth(summed, 1), 2) / 2.0
    entry = table_entries(tf_table, tf_index)
    emit, transmit = shade(grad_z, grad_x, grad_y, density, entry, step_len)
    front_local, brick_trans = front_products(transmit)
    brick_color = jnp.sum(front_local[None] * emit, axis=1)
    front = entering(
        brick_trans, "depth", lambda earlier, later: earlier * later, jnp.ones_like(brick_trans)
    )
    terms = jnp.concatenate(
        [front[None] * brick_color, (front * (1.0 - brick_trans))[None]], axis=0
    )
    image = lax.psum_scatter(terms, "depth", scatter_dimension=2, tiled=True)
    return image


def solution(mesh):
    in_specs = (P("depth", "gx", None), P("depth", "gx", None), P())
    out_specs = P(None, "gx", "depth")
    return jax.shard_map(body, mesh=mesh, in_specs=in_specs, out_specs=out_specs, check_vma=False)
```

profile of v0, /device:TPU:0, one launch (start us, length us, event | category | flops | bytes accessed | tf_op | source)
XLA Modules:
  0.0 147.1 jit_solution(10444240548824449368)
XLA Ops:
  6.5 0.8 fusion.27
  7.4 1.3 collective-permute-start.1
  8.7 3.0 %collective-permute-start = (f32[1,8,1024]{2,1,0:T(8,128)S(1)}, f32[1,8,1024]{2,1,0:T(8,128)S(1)}, u32[]{:S(2)}, u32[]{:S(2)}) collective-permute-start(f32[1,8,1024]{2,1,0:T(8,128)S(1)} %get-tuple-element.163), channel_id=1, source_target_pairs={{0,2},{2,4},{4,6},{6,8},{8,10},{10,12},{12,14},{14,16},{16,18},{18... | collective-permute-start | bytes 98312 | tf_op jit(solution)/shard_map/ppermute | solution.py:15
  11.7 36.3 %while.25 = (s32[]{:T(128)}, f32[16,4,1024]{2,0,1:T(8,128)S(1)}, s32[16,1024]{1,0:T(8,128)}, f32[4,256]{1,0:T(4,128)}, s32[]{:T(128)}, /*index=5*/s32[]{:T(128)}) while((s32[]{:T(128)}, f32[16,4,1024]{2,0,1:T(8,128)S(1)}, s32[16,1024]{1,0:T(8,128)}, f32[4,256]{1,0:T(4,128)}, s32[]{:T(128)}, /*index=5*/s32[]{:T(128)}) %tuple.62), condition=%wide.region_1.2_spmd.clone, body=%wide.region_0.1_spmd.clone.sunk | while | flops 12845058 | bytes 98389 | solution.py:89
  11.7 0.8 constant_dynamic-slice_fusion.2
  12.5 1.3 convolution_bitcast_fusion.2
  14.0 0.8 constant_dynamic-slice_fusion.2
  14.8 1.3 convolution_bitcast_fusion.2
  16.3 0.8 constant_dynamic-slice_fusion.2
  17.1 1.3 convolution_bitcast_fusion.2
  18.6 0.8 constant_dynamic-slice_fusion.2
  19.3 1.3 convolution_bitcast_fusion.2
  20.8 0.8 constant_dynamic-slice_fusion.2
  21.6 1.3 convolution_bitcast_fusion.2
  23.1 0.8 constant_dynamic-slice_fusion.2
  23.9 1.3 convolution_bitcast_fusion.2
  25.4 0.8 constant_dynamic-slice_fusion.2
  26.1 1.3 convolution_bitcast_fusion.2
  27.6 0.8 constant_dynamic-slice_fusion.2
  28.4 1.3 convolution_bitcast_fusion.2
  29.9 0.8 constant_dynamic-slice_fusion.2
  30.7 1.3 convolution_bitcast_fusion.2
  32.2 0.8 constant_dynamic-slice_fusion.2
  33.0 1.3 convolution_bitcast_fusion.2
  34.5 0.8 constant_dynamic-slice_fusion.2
  35.2 1.3 convolution_bitcast_fusion.2
  36.7 0.8 constant_dynamic-slice_fusion.2
  37.5 1.3 convolution_bitcast_fusion.2
  39.0 0.8 constant_dynamic-slice_fusion.2
  39.8 1.3 convolution_bitcast_fusion.2
  41.3 0.8 constant_dynamic-slice_fusion.2
  42.0 1.3 convolution_bitcast_fusion.2
  43.5 0.8 constant_dynamic-slice_fusion.2
  44.3 1.3 convolution_bitcast_fusion.2
  45.8 0.8 constant_dynamic-slice_fusion.2
  46.6 1.3 convolution_bitcast_fusion.2
  48.1 0.9 fusion.18
  49.0 24.6 %all_gather.3 = f32[16,8,1024]{2,1,0:T(8,128)S(1)} all-gather(f32[1,8,1024]{2,1,0:T(8,128)S(1)} %get-tuple-element.161), channel_id=1, replica_groups=mesh['depth'=16,'gx'=2] {'depth'}, dimensions={0}, use_global_device_ids=true | all-gather | bytes 557056 | tf_op jit(solution)/shard_map/all_gather | solution.py:26
  73.5 0.6 while.26
  74.2 3.4 %collective-permute-start.2 = (f32[4,1,1024]{2,1,0:T(1,128)S(1)}, f32[4,1,1024]{2,1,0:T(1,128)S(1)}, u32[]{:S(2)}, u32[]{:S(2)}) collective-permute-start(f32[4,1,1024]{2,1,0:T(1,128)S(1)} %get-tuple-element.158), channel_id=1, source_target_pairs={{0,1},{2,3},{4,5},{6,7},{8,9},{10,11},{12,13},{14,15},{16,17},{18,... | collective-permute-start | bytes 49160 | tf_op jit(solution)/shard_map/ppermute | solution.py:15
  77.7 1.3 collective-permute-start.3
  79.1 4.2 %collective-permute-done.3 = f32[4,1,1024]{2,1,0:T(1,128)S(1)} collective-permute-done((f32[4,1,1024]{2,1,0:T(1,128)S(1)}, f32[4,1,1024]{2,1,0:T(1,128)S(1)}, u32[]{:S(2)}, u32[]{:S(2)}) %collective-permute-start.3) | collective-permute-done | bytes 16416 | tf_op jit(solution)/shard_map/ppermute | solution.py:17
  83.3 0.2 select_maximum_fusion
  83.9 0.8 copy.6
  84.7 1.7 %reshape.17 = f32[1024,32]{1,0:T(8,128)} reshape(f32[1024,4,8]{2,1,0:T(4,128)S(1)} %bitcast.43) | data formatting | bytes 262144
  86.4 52.2 %reduce-scatter.4.cloned.1.call-done = f32[64,32]{1,0:T(8,128)} async-done(((f32[1024,32]{1,0:T(8,128)}), f32[64,32]{1,0:T(8,128)}) %reduce-scatter.4.cloned.1.call-update) | async-done | bytes 8208
  138.7 0.9 reshape.18
  139.5 0.7 copy.7
  (70 shorter events, 3.6 us)
Async XLA Ops:
  6.5 67.6 %copy-start = (f32[2,8,1024]{2,1,0:T(8,128)S(1)}, f32[2,8,1024]{2,1,0:T(8,128)}, u32[]{:S(2)}) copy-start(f32[2,8,1024]{2,1,0:T(8,128)} %param.7) | copy-start | bytes 196612
  6.5 132.1 %reduce-scatter.4.cloned.1.call-start = ((), (), s32[]{:S(2)}) async-start(), calls=%async_computation.1 | async-start | bytes 557056
  7.4 66.8 %collective-permute-start.1 = (f32[1,8,1024]{2,1,0:T(8,128)S(1)}, f32[1,8,1024]{2,1,0:T(8,128)S(1)}, u32[]{:S(2)}, u32[]{:S(2)}) collective-permute-start(f32[1,8,1024]{2,1,0:T(8,128)S(1)} %get-tuple-element.162), channel_id=1, source_target_pairs={{2,0},{4,2},{6,4},{8,6},{10,8},{12,10},{14,12},{16,14},{18,16},{20... | collective-permute-start | bytes 98312 | tf_op jit(solution)/shard_map/ppermute | solution.py:17
  8.7 65.5 %collective-permute-start = (f32[1,8,1024]{2,1,0:T(8,128)S(1)}, f32[1,8,1024]{2,1,0:T(8,128)S(1)}, u32[]{:S(2)}, u32[]{:S(2)}) collective-permute-start(f32[1,8,1024]{2,1,0:T(8,128)S(1)} %get-tuple-element.163), channel_id=1, source_target_pairs={{0,2},{2,4},{4,6},{6,8},{8,10},{10,12},{12,14},{14,16},{16,18},{18... | collective-permute-start | bytes 98312 | tf_op jit(solution)/shard_map/ppermute | solution.py:15
  74.2 4.9 %collective-permute-start.2 = (f32[4,1,1024]{2,1,0:T(1,128)S(1)}, f32[4,1,1024]{2,1,0:T(1,128)S(1)}, u32[]{:S(2)}, u32[]{:S(2)}) collective-permute-start(f32[4,1,1024]{2,1,0:T(1,128)S(1)} %get-tuple-element.158), channel_id=1, source_target_pairs={{0,1},{2,3},{4,5},{6,7},{8,9},{10,11},{12,13},{14,15},{16,17},{18,... | collective-permute-start | bytes 49160 | tf_op jit(solution)/shard_map/ppermute | solution.py:15
  77.7 5.6 %collective-permute-start.3 = (f32[4,1,1024]{2,1,0:T(1,128)S(1)}, f32[4,1,1024]{2,1,0:T(1,128)S(1)}, u32[]{:S(2)}, u32[]{:S(2)}) collective-permute-start(f32[4,1,1024]{2,1,0:T(1,128)S(1)} %get-tuple-element.159), channel_id=1, source_target_pairs={{1,0},{3,2},{5,4},{7,6},{9,8},{11,10},{13,12},{15,14},{17,16},{19,... | collective-permute-start | bytes 49160 | tf_op jit(solution)/shard_map/ppermute | solution.py:17
Sparse Core Ops, SparseCore 0:
  86.5 52.0 reduce-scatter.3
where the time goes:
time: 149 us; the launch traced here: 147 us
  waiting for transfers between devices  56.5 us (38%)
  blocking collectives  24.6 us (17%)
  matrix products  20.6 us (14%)
  local copies, waits for them, and re-layouts  20.2 us (14%)
  between operations  13.6 us (9%)
  starting transfers between devices  9.03 us (6%)
  other arithmetic  1.59 us (1%)
    unnamed x2, waiting for transfers between devices  52.2 us
    all_gather x1, blocking collectives, entering(): everything = lax.all_gather(array, axis)  24.6 us
    dot_general x16, matrix products, lookup(): lax.dot_general(tf_table, onehot, (((1,), (1,)), ((), ())), precision=lax...  20.6 us
    dynamic_slice x16, local copies, waits for them, and re-layouts, table_entries(): looked = lax.map(lookup, rows)  12.3 us
    ppermute x2, starting transfers between devices, extended(): lax.ppermute(tail, axis, [(i, (i + 1) % count) for i in range(ends)])  6.46 us
    ppermute x2, waiting for transfers between devices, extended(): lax.ppermute(head, axis, [((i + 1) % count, i) for i in range(ends)])  4.21 us
    unnamed x8, local copies, waits for them, and re-layouts  4.1 us
  transfers between devices with their start and end apart: 5, of which 3 were waited for; matrix products, arithmetic and copies ran while one was open for 25% of the time, Pallas kernels for 0%

commit v1 on v0

v1 whole, which is shorter than its diff:
```python
import functools

import jax
import jax.numpy as jnp
from jax import lax
from jax.experimental import pallas as pl
from jax.experimental.pallas import tpu as pltpu
from jax.sharding import PartitionSpec as P

LANES = 128
ROWS = 8
BLOCK = 3 * ROWS
WHOLE = pl.BlockSpec(memory_space=pltpu.VMEM)


def pack_kernel(width, dens_ref, index_ref, out_ref):
    length = dens_ref.shape[2]
    lane = lax.broadcasted_iota(jnp.int32, (ROWS, LANES), 1)
    column = lax.broadcasted_iota(jnp.int32, (ROWS, length), 1)
    dens = [dens_ref[0], dens_ref[1]]
    index = [index_ref[0].astype(jnp.float32), index_ref[1].astype(jnp.float32)]
    before = [jnp.where(column == 0, 0.0, pltpu.roll(d, 1, 1)) for d in dens]
    after = [jnp.where(column == length - 1, 0.0, pltpu.roll(d, length - 1, 1)) for d in dens]

    def block(pair, j):
        start = (width * j) // LANES * LANES
        shift = width * j - start
        layers = []
        for layer, value in enumerate(pair):
            amount = (layer * width - shift) % LANES
            window = value[:, start : start + LANES]
            layers.append(pltpu.roll(window, amount, 1) if amount else window)
        return jnp.where(lane < width, layers[0], layers[1])

    for j in range(length // width):
        out_ref[j, 0:ROWS] = block(dens, j)
        out_ref[j, ROWS : 2 * ROWS] = block(index, j)
        out_ref[j, 2 * ROWS : 3 * ROWS] = jnp.where(
            lane % width == 0, block(before, j), block(after, j)
        )


def edge_kernel(got_ref, low_ref, high_ref):
    low_ref[0] = got_ref[:, 0, :]
    low_ref[1] = got_ref[:, 2 * ROWS, :]
    high_ref[0] = got_ref[:, ROWS - 1, :]
    high_ref[1] = got_ref[:, 3 * ROWS - 1, :]


def edge_pick_kernel(got_ref, edge_ref):
    first = lax.axis_index("gx") == 0
    edge_ref[0] = jnp.where(first, got_ref[:, ROWS - 1, :], got_ref[:, 0, :])
    edge_ref[1] = jnp.where(first, got_ref[:, 3 * ROWS - 1, :], got_ref[:, 2 * ROWS, :])


def trade(value, lane, width):
    if 2 * width == LANES:
        return pltpu.roll(value, width, 1)
    return jnp.where(lane < width, pltpu.roll(value, LANES - width, 1), pltpu.roll(value, width, 1))


def render_kernel(width, step_len, paired, got_ref, *refs):
    edge_refs, (table_ref, out_ref) = refs[:-2], refs[-2:]
    bricks = got_ref.shape[0]
    levels = table_ref.shape[1]
    lane = lax.broadcasted_iota(jnp.int32, (ROWS, LANES), 1)
    row = lax.broadcasted_iota(jnp.int32, (ROWS, LANES), 0)
    front_layer = lane < width

    def edge_parts(values):
        brick = lax.broadcasted_iota(jnp.int32, (bricks, LANES), 0)
        edge_lane = lax.broadcasted_iota(jnp.int32, (bricks, LANES), 1)
        other = trade(values, edge_lane, width)
        later = jnp.where(brick == bricks - 1, 0.0, pltpu.roll(other, bricks - 1, 0))
        earlier = jnp.where(brick == 0, 0.0, pltpu.roll(other, 1, 0))
        behind = jnp.where(edge_lane < width, other, later)
        ahead = jnp.where(edge_lane < width, earlier, other)
        return (behind - ahead, ahead + 2.0 * values + behind)

    if paired:
        first = lax.axis_index("gx") == 0
        here = [edge_refs[0][part] for part in range(2)]
        zero = jnp.zeros_like(here[0])
        low = [jnp.where(first, zero, value) for value in here]
        high = [jnp.where(first, value, zero) for value in here]
    else:
        low = [edge_refs[0][part] for part in range(2)]
        high = [edge_refs[1][part] for part in range(2)]
    low = [edge_parts(value) for value in low]
    high = [edge_parts(value) for value in high]

    table = [
        [
            jnp.broadcast_to(table_ref[c : c + 1, start : start + LANES], (ROWS, LANES))
            for start in range(0, levels, LANES)
        ]
        for c in range(4)
    ]

    def lookup(parts, index):
        within = index & (LANES - 1)
        value = jnp.take_along_axis(parts[0], within, axis=1, mode="promise_in_bounds")
        for k in range(1, len(parts)):
            more = jnp.take_along_axis(parts[k], within, axis=1, mode="promise_in_bounds")
            value = jnp.where(index >= k * LANES, more, value)
        return value

    zero = jnp.zeros((ROWS, LANES), jnp.float32)
    dens = [got_ref[k, 0:ROWS] for k in range(bricks)]
    side = [got_ref[k, 2 * ROWS : 3 * ROWS] for k in range(bricks)]
    dens_other = [zero] + [trade(value, lane, width) for value in dens] + [zero]
    side_other = [zero] + [trade(value, lane, width) for value in side] + [zero]

    def depth_parts(value, other, k):
        behind = jnp.where(front_layer, other[k + 1], other[k + 2])
        ahead = jnp.where(front_layer, other[k], other[k + 1])
        return (behind - ahead, ahead + 2.0 * value + behind)

    def across(value, k, part, which):
        below = jnp.where(row == 0, low[part][which][k : k + 1], pltpu.roll(value, 1, 0))
        above = jnp.where(row == ROWS - 1, high[part][which][k : k + 1], pltpu.roll(value, ROWS - 1, 0))
        return below, above

    front = jnp.ones((ROWS, LANES), jnp.float32)
    image = [zero, zero, zero]
    for k in range(bricks):
        planes = []
        for part, (values, other) in enumerate(((dens, dens_other), (side, side_other))):
            delta, total = depth_parts(values[k], other, k)
            below, above = across(delta, k, part, 0)
            for_z = below + 2.0 * delta + above
            below, above = across(total, k, part, 1)
            planes.append((for_z, above - below, below + 2.0 * total + above))

        def beside(which):
            inner, outer = planes[0][which], planes[1][which]
            before = jnp.where(lane % width == 0, outer, pltpu.roll(inner, 1, 1))
            after = jnp.where(lane % width == width - 1, outer, pltpu.roll(inner, LANES - 1, 1))
            return before, inner, after

        before, inner, after = beside(0)
        grad_z = (before + 2.0 * inner + after) * 0.5
        before, inner, after = beside(1)
        grad_x = (before + 2.0 * inner + after) * 0.5
        before, _, after = beside(2)
        grad_y = (after - before) * 0.5

        inverse = lax.rsqrt(grad_z * grad_z + grad_x * grad_x + grad_y * grad_y + 1.0)
        ndl = (0.48 * grad_z + 0.6 * grad_x + 0.64 * grad_y) * inverse
        ndh = (0.86023 * grad_z + 0.34875 * grad_x + 0.372 * grad_y) * inverse
        shine = jnp.maximum(ndh, 0.0)
        shine = shine * shine
        shine = shine * shine
        shine = shine * shine
        lit = 0.3 + 0.6 * jnp.abs(ndl) + 0.4 * shine

        index = got_ref[k, ROWS : 2 * ROWS].astype(jnp.int32)
        alpha = 1.0 - jnp.exp(-lookup(table[3], index) * dens[k] * step_len)
        transmit = 1.0 - alpha
        transmit_other = trade(transmit, lane, width)
        weight = jnp.where(front_layer, front, front * transmit_other) * (alpha * lit)
        image = [image[c] + weight * lookup(table[c], index) for c in range(3)]
        front = front * (transmit * transmit_other)

    for c in range(3):
        out_ref[c] = (image[c] + trade(image[c], lane, width))[:, :width]
    out_ref[3] = (1.0 - front)[:, :width]


def body(density, tf_index, tf_table):
    bricks, ranks = lax.axis_size("depth"), lax.axis_size("gx")
    layers, rows, length = density.shape
    width = length // bricks
    assert layers == 2 and rows == ROWS and 2 * width <= LANES and LANES % width == 0
    step_len = 1.0 / (layers * bricks)
    packed = pl.pallas_call(
        functools.partial(pack_kernel, width),
        out_shape=jax.ShapeDtypeStruct((bricks, BLOCK, LANES), jnp.float32),
        in_specs=[WHOLE] * 2,
        out_specs=WHOLE,
        name="pack",
    )(density, tf_index)
    got = lax.all_to_all(packed, "depth", 0, 0, tiled=True)
    edge = jax.ShapeDtypeStruct((2, bricks, LANES), jnp.float32)
    paired = ranks == 2
    if paired:
        mine = pl.pallas_call(
            edge_pick_kernel, out_shape=edge, in_specs=[WHOLE], out_specs=WHOLE, name="edge"
        )(got)
        edges = [lax.ppermute(mine, "gx", [(0, 1), (1, 0)])]
    else:
        first, last = pl.pallas_call(
            edge_kernel, out_shape=[edge] * 2, in_specs=[WHOLE], out_specs=[WHOLE] * 2, name="edge"
        )(got)
        edges = [
            lax.ppermute(last, "gx", [(i, i + 1) for i in range(ranks - 1)]),
            lax.ppermute(first, "gx", [(i + 1, i) for i in range(ranks - 1)]),
        ]
    return pl.pallas_call(
        functools.partial(render_kernel, width, step_len, paired),
        out_shape=jax.ShapeDtypeStruct((4, rows, width), jnp.float32),
        in_specs=[WHOLE] * (2 + len(edges)),
        out_specs=WHOLE,
        name="render",
    )(got, *edges, tf_table)


def solution(mesh):
    in_specs = (P("depth", "gx", None), P("depth", "gx", None), P())
    out_specs = P(None, "gx", "depth")
    return jax.shard_map(body, mesh=mesh, in_specs=in_specs, out_specs=out_specs, check_vma=False)
```

time: 149 us -> 27.4 us (0.18); the launches traced: 147 us -> 27.1 us
  waiting for transfers between devices: 56.5 us -> 2.43 us
  matrix products: 20.6 us -> 0 us
  local copies, waits for them, and re-layouts: 20.2 us -> 0.6 us
  between operations: 13.6 us -> 0.01 us
  blocking collectives: 24.6 us -> 16.4 us
  starting transfers between devices: 9.03 us -> 1.52 us
  Pallas kernels: 0 us -> 6.09 us
  other arithmetic: 1.59 us -> 0 us
    unnamed x2 -> x0, waiting for transfers between devices: 52.2 us -> none
    all_gather x1 -> x0, blocking collectives: 24.6 us -> none  [entering(): everything = lax.all_gather(array, axis)]
    dot_general x16 -> x0, matrix products: 20.6 us -> none  [lookup(): lax.dot_general(tf_table, onehot, (((1,), (1,)), ((), ())), precision=lax...]
    all_to_all x0 -> x1, blocking collectives: none -> 16.4 us  [body(): got = lax.all_to_all(packed, 'depth', 0, 0, tiled=True)]
    dynamic_slice x16 -> x0, local copies, waits for them, and re-layouts: 12.3 us -> none  [table_entries(): looked = lax.map(lookup, rows)]
    ppermute x4 -> x1, starting transfers between devices: 9.03 us -> 1.52 us  [body(): edges = [lax.ppermute(mine, 'gx', [(0, 1), (1, 0)])]]
    pallas_call x0 -> x3, Pallas kernels: none -> 6.09 us  [the longest x1 2.77 us: body(): pl.pallas_call(functools.partial(render_kernel, width, step_len, paired),...]
    unnamed x8 -> x2, local copies, waits for them, and re-layouts: 4.1 us -> 0.6 us
  transfers between devices with their start and end apart: 5 -> 1, of which waited for: 3 -> 1; matrix products, arithmetic and copies ran while one was open for 25% -> 0% of each run, Pallas kernels for 0% -> 0%
where the time goes in v1:
time: 27.4 us; the launch traced here: 27.1 us
  blocking collectives  16.4 us (60%)
  Pallas kernels  6.09 us (22%)
  waiting for transfers between devices  2.43 us (9%)
  starting transfers between devices  1.52 us (6%)
  local copies, waits for them, and re-layouts  0.6 us (2%)
    all_to_all x1, blocking collectives, body(): got = lax.all_to_all(packed, 'depth', 0, 0, tiled=True)  16.4 us
    pallas_call x1, Pallas kernels, body(): pl.pallas_call(functools.partial(render_kernel, width, step_len, paired),...  2.77 us
    ppermute x1, waiting for transfers between devices, body(): edges = [lax.ppermute(mine, 'gx', [(0, 1), (1, 0)])]  2.43 us
    pallas_call x1, Pallas kernels, body(): pl.pallas_call(functools.partial(pack_kernel, width), out_shape=jax.Shape...  1.76 us
    pallas_call x1, Pallas kernels, body(): pl.pallas_call(edge_pick_kernel, out_shape=edge, in_specs=[WHOLE], out_sp...  1.56 us
    ppermute x1, starting transfers between devices, body(): edges = [lax.ppermute(mine, 'gx', [(0, 1), (1, 0)])]  1.52 us
    unnamed x2, local copies, waits for them, and re-layouts  0.6 us
  transfers between devices with their start and end apart: 1, of which 1 were waited for; matrix products, arithmetic and copies ran while one was open for 0% of the time, Pallas kernels for 0%

profile of v1, /device:TPU:0, one launch (start us, length us, event | category | flops | bytes accessed | tf_op | source)
XLA Modules:
  0.0 27.1 jit_solution(4448860862805759594)
XLA Ops:
  0.0 1.8 %pack.1 = f32[16,24,128]{2,1,0:T(8,128)} custom-call(f32[2,8,1024]{2,1,0:T(8,128)} %dens_ref.1, s32[2,8,1024]{2,1,0:T(8,128)} %index_ref.1), custom_call_target="tpu_custom_call" | custom-call | tf_op jit(solution)/shard_map/pack/pallas_call | solution.py:176
  1.8 16.4 %all_to_all.5.got_ref = f32[16,24,128]{2,1,0:T(8,128)} all-to-all(f32[16,24,128]{2,1,0:T(8,128)} %pack.1), channel_id=1, replica_groups=mesh['depth'=16,'gx'=2] {'depth'}, dimensions={0} | all-to-all | bytes 393216 | tf_op jit(solution)/shard_map/all_to_all | solution.py:183
  18.2 1.6 %edge.1 = f32[2,16,128]{2,1,0:T(8,128)} custom-call(f32[16,24,128]{2,1,0:T(8,128)} %all_to_all.5.got_ref), custom_call_target="tpu_custom_call" | custom-call | tf_op jit(solution)/shard_map/edge/pallas_call | solution.py:187
  19.8 1.5 %collective-permute-start = (f32[2,16,128]{2,1,0:T(8,128)}, f32[2,16,128]{2,1,0:T(8,128)S(1)}, u32[]{:S(2)}, u32[]{:S(2)}) collective-permute-start(f32[2,16,128]{2,1,0:T(8,128)} %edge.1), channel_id=1, source_target_pairs={{0,1},{1,0},{2,3},{3,2},{4,5},{5,4},{6,7},{7,6},{8,9},{9,8},{10,11... | collective-permute-start | bytes 49160 | tf_op jit(solution)/shard_map/ppermute | solution.py:190
  21.3 2.4 %collective-permute-done.refs_0_ = f32[2,16,128]{2,1,0:T(8,128)S(1)} collective-permute-done((f32[2,16,128]{2,1,0:T(8,128)}, f32[2,16,128]{2,1,0:T(8,128)S(1)}, u32[]{:S(2)}, u32[]{:S(2)}) %collective-permute-start) | collective-permute-done | bytes 16416 | tf_op jit(solution)/shard_map/ppermute | solution.py:190
  23.7 0.0 copy-start
  23.7 0.6 %copy-done = f32[2,16,128]{2,1,0:T(8,128)} copy-done((f32[2,16,128]{2,1,0:T(8,128)}, f32[2,16,128]{2,1,0:T(8,128)S(1)}, u32[]{:S(2)}) %copy-start) | copy-done | bytes 16408
  24.3 2.8 %render.1 = f32[4,8,64]{2,1,0:T(8,128)} custom-call(f32[16,24,128]{2,1,0:T(8,128)} %all_to_all.5.got_ref, f32[2,16,128]{2,1,0:T(8,128)} %copy-done, f32[4,256]{1,0:T(4,128)} %refs_1_.1), custom_call_target="tpu_custom_call" | custom-call | tf_op jit(solution)/shard_map/render/pallas_call | solution.py:199
Async XLA Ops:
  19.8 3.9 %collective-permute-start = (f32[2,16,128]{2,1,0:T(8,128)}, f32[2,16,128]{2,1,0:T(8,128)S(1)}, u32[]{:S(2)}, u32[]{:S(2)}) collective-permute-start(f32[2,16,128]{2,1,0:T(8,128)} %edge.1), channel_id=1, source_target_pairs={{0,1},{1,0},{2,3},{3,2},{4,5},{5,4},{6,7},{7,6},{8,9},{9,8},{10,11... | collective-permute-start | bytes 49160 | tf_op jit(solution)/shard_map/ppermute | solution.py:190
  23.7 0.6 %copy-start = (f32[2,16,128]{2,1,0:T(8,128)}, f32[2,16,128]{2,1,0:T(8,128)S(1)}, u32[]{:S(2)}) copy-start(f32[2,16,128]{2,1,0:T(8,128)S(1)} %collective-permute-done.refs_0_) | copy-start | bytes 49156

commit v2 on v1

--- a/solution.py
+++ b/solution.py
@@ -11,9 +11,16 @@
 ROWS = 8
 BLOCK = 3 * ROWS
 WHOLE = pl.BlockSpec(memory_space=pltpu.VMEM)
-
-
-def pack_kernel(width, dens_ref, index_ref, out_ref):
+PARAMS = pltpu.CompilerParams(vmem_limit_bytes=4 << 20)
+
+
+def pack_kernel(width, dens_hbm, index_hbm, out_ref, dens_ref, index_ref, dens_sem, index_sem):
+    dens_copy = pltpu.make_async_copy(dens_hbm, dens_ref, dens_sem)
+    index_copy = pltpu.make_async_copy(index_hbm, index_ref, index_sem)
+    dens_copy.start()
+    index_copy.start()
+    dens_copy.wait()
+    index_copy.wait()
     length = dens_ref.shape[2]
     lane = lax.broadcasted_iota(jnp.int32, (ROWS, LANES), 1)
     column = lax.broadcasted_iota(jnp.int32, (ROWS, length), 1)
@@ -176,21 +183,27 @@
     packed = pl.pallas_call(
         functools.partial(pack_kernel, width),
         out_shape=jax.ShapeDtypeStruct((bricks, BLOCK, LANES), jnp.float32),
-        in_specs=[WHOLE] * 2,
+        in_specs=[pl.BlockSpec(memory_space=pltpu.HBM)] * 2,
         out_specs=WHOLE,
-        name="pack",
-    )(density, tf_index)
+        scratch_shapes=[
+            pltpu.VMEM(density.shape, density.dtype),
+            pltpu.VMEM(tf_index.shape, tf_index.dtype),
+            pltpu.SemaphoreType.DMA,
+            pltpu.SemaphoreType.DMA,
+        ],
+        name="pack", compiler_params=PARAMS,
+    )(*(pltpu.with_memory_space_constraint(a, pltpu.HBM) for a in (density, tf_index)))
     got = lax.all_to_all(packed, "depth", 0, 0, tiled=True)
     edge = jax.ShapeDtypeStruct((2, bricks, LANES), jnp.float32)
     paired = ranks == 2
     if paired:
         mine = pl.pallas_call(
-            edge_pick_kernel, out_shape=edge, in_specs=[WHOLE], out_specs=WHOLE, name="edge"
+            edge_pick_kernel, out_shape=edge, in_specs=[WHOLE], out_specs=WHOLE, name="edge", compiler_params=PARAMS
         )(got)
         edges = [lax.ppermute(mine, "gx", [(0, 1), (1, 0)])]
     else:
         first, last = pl.pallas_call(
-            edge_kernel, out_shape=[edge] * 2, in_specs=[WHOLE], out_specs=[WHOLE] * 2, name="edge"
+            edge_kernel, out_shape=[edge] * 2, in_specs=[WHOLE], out_specs=[WHOLE] * 2, name="edge", compiler_params=PARAMS
         )(got)
         edges = [
             lax.ppermute(last, "gx", [(i, i + 1) for i in range(ranks - 1)]),
@@ -201,7 +214,7 @@
         out_shape=jax.ShapeDtypeStruct((4, rows, width), jnp.float32),
         in_specs=[WHOLE] * (2 + len(edges)),
         out_specs=WHOLE,
-        name="render",
+        name="render", compiler_params=PARAMS,
     )(got, *edges, tf_table)
 
 

time: 27.4 us -> 23.1 us (0.84)
  Pallas kernels: 6.09 us -> 2.95 us
  local copies, waits for them, and re-layouts: 0.6 us -> 0.01 us
  blocking collectives: 16.4 us -> 16.1 us
    pallas_call x1, Pallas kernels: 1.56 us -> 0.02 us  [body(): pl.pallas_call(edge_pick_kernel, out_shape=edge, in_specs=[WHOLE], out_sp...]
    pallas_call x1, Pallas kernels: 2.77 us -> 1.83 us  [body(): pl.pallas_call(functools.partial(render_kernel, width, step_len, paired),...]
    pallas_call x1, Pallas kernels: 1.76 us -> 1.1 us  [body(): pl.pallas_call(functools.partial(pack_kernel, width), out_shape=jax.Shape...]
    unnamed x2, local copies, waits for them, and re-layouts: 0.6 us -> 0.01 us
    all_to_all x1, blocking collectives: 16.4 us -> 16.1 us  [body(): got = lax.all_to_all(packed, 'depth', 0, 0, tiled=True)]
where the time goes in v2:
time: 23.1 us; the launch traced here: 22.9 us
  blocking collectives  16.1 us (70%)
  Pallas kernels  2.95 us (13%)
  waiting for transfers between devices  2.22 us (10%)
  starting transfers between devices  1.58 us (7%)
    all_to_all x1, blocking collectives, body(): got = lax.all_to_all(packed, 'depth', 0, 0, tiled=True)  16.1 us
    ppermute x1, waiting for transfers between devices, body(): edges = [lax.ppermute(mine, 'gx', [(0, 1), (1, 0)])]  2.22 us
    pallas_call x1, Pallas kernels, body(): pl.pallas_call(functools.partial(render_kernel, width, step_len, paired),...  1.83 us
    ppermute x1, starting transfers between devices, body(): edges = [lax.ppermute(mine, 'gx', [(0, 1), (1, 0)])]  1.58 us
    pallas_call x1, Pallas kernels, body(): pl.pallas_call(functools.partial(pack_kernel, width), out_shape=jax.Shape...  1.1 us
  transfers between devices with their start and end apart: 1, of which 1 were waited for; matrix products, arithmetic and copies ran while one was open for 0% of the time, Pallas kernels for 0%

profile of v2, /device:TPU:0, one launch (start us, length us, event | category | flops | bytes accessed | tf_op | source)
XLA Modules:
  0.0 22.9 jit_solution(8655375117547356766)
XLA Ops:
  0.0 1.1 %pack.1 = f32[16,24,128]{2,1,0:T(8,128)S(1)} custom-call(f32[2,8,1024]{2,1,0:T(8,128)} %dens_hbm.1, s32[2,8,1024]{2,1,0:T(8,128)} %index_hbm.1), custom_call_target="tpu_custom_call" | custom-call | tf_op jit(solution)/shard_map/pack/pallas_call | solution.py:183
  1.1 16.1 %all_to_all.5.got_ref = f32[16,24,128]{2,1,0:T(8,128)S(1)} all-to-all(f32[16,24,128]{2,1,0:T(8,128)S(1)} %pack.1), channel_id=1, replica_groups=mesh['depth'=16,'gx'=2] {'depth'}, dimensions={0} | all-to-all | bytes 393216 | tf_op jit(solution)/shard_map/all_to_all | solution.py:196
  17.3 0.0 copy-start
  17.3 1.6 %collective-permute-start = (f32[2,16,128]{2,1,0:T(8,128)S(1)}, f32[2,16,128]{2,1,0:T(8,128)S(1)}, u32[]{:S(2)}, u32[]{:S(2)}) collective-permute-start(f32[2,16,128]{2,1,0:T(8,128)S(1)} %edge.1), channel_id=1, source_target_pairs={{0,1},{1,0},{2,3},{3,2},{4,5},{5,4},{6,7},{7,6},{8,9},{9,8},{10,11... | collective-permute-start | bytes 49160 | tf_op jit(solution)/shard_map/ppermute | solution.py:203
  18.9 2.2 %collective-permute-done.refs_0_ = f32[2,16,128]{2,1,0:T(8,128)S(1)} collective-permute-done((f32[2,16,128]{2,1,0:T(8,128)S(1)}, f32[2,16,128]{2,1,0:T(8,128)S(1)}, u32[]{:S(2)}, u32[]{:S(2)}) %collective-permute-start) | collective-permute-done | bytes 16416 | tf_op jit(solution)/shard_map/ppermute | solution.py:203
  21.1 0.0 copy-done
  21.1 1.8 %render.1 = f32[4,8,64]{2,1,0:T(8,128)} custom-call(f32[16,24,128]{2,1,0:T(8,128)S(1)} %all_to_all.5.got_ref, f32[2,16,128]{2,1,0:T(8,128)S(1)} %collective-permute-done.refs_0_, f32[4,256]{1,0:T(4,128)S(1)} %copy-done), custom_call_target="tpu_custom_call" | custom-call | tf_op jit(solution)/shard_map/render/pallas_call | solution.py:212
  (1 shorter events, 0.0 us)
Async XLA Ops:
  17.3 3.8 %copy-start = (f32[4,256]{1,0:T(4,128)S(1)}, f32[4,256]{1,0:T(4,128)}, u32[]{:S(2)}) copy-start(f32[4,256]{1,0:T(4,128)} %refs_1_.1) | copy-start | bytes 12292
  17.3 3.8 %collective-permute-start = (f32[2,16,128]{2,1,0:T(8,128)S(1)}, f32[2,16,128]{2,1,0:T(8,128)S(1)}, u32[]{:S(2)}, u32[]{:S(2)}) collective-permute-start(f32[2,16,128]{2,1,0:T(8,128)S(1)} %edge.1), channel_id=1, source_target_pairs={{0,1},{1,0},{2,3},{3,2},{4,5},{5,4},{6,7},{7,6},{8,9},{9,8},{10,11... | collective-permute-start | bytes 49160 | tf_op jit(solution)/shard_map/ppermute | solution.py:203

commit v3 on v2

v3 whole, which is shorter than its diff:
```python
import functools

import jax
import jax.numpy as jnp
from jax import lax
from jax.experimental import pallas as pl
from jax.experimental.pallas import tpu as pltpu
from jax.sharding import PartitionSpec as P

LANES = 128
ROWS = 8
BLOCK = 3 * ROWS
WHOLE = pl.BlockSpec(memory_space=pltpu.VMEM)
PARAMS = pltpu.CompilerParams(vmem_limit_bytes=4 << 20)


def pack_kernel(width, dens_hbm, index_hbm, out_ref, dens_ref, index_ref, dens_sem, index_sem):
    dens_copy = pltpu.make_async_copy(dens_hbm, dens_ref, dens_sem)
    index_copy = pltpu.make_async_copy(index_hbm, index_ref, index_sem)
    dens_copy.start()
    index_copy.start()
    dens_copy.wait()
    index_copy.wait()
    length = dens_ref.shape[2]
    lane = lax.broadcasted_iota(jnp.int32, (ROWS, LANES), 1)
    column = lax.broadcasted_iota(jnp.int32, (ROWS, length), 1)
    dens = [dens_ref[0], dens_ref[1]]
    index = [index_ref[0].astype(jnp.float32), index_ref[1].astype(jnp.float32)]
    before = [jnp.where(column == 0, 0.0, pltpu.roll(d, 1, 1)) for d in dens]
    after = [jnp.where(column == length - 1, 0.0, pltpu.roll(d, length - 1, 1)) for d in dens]

    def block(pair, j):
        start = (width * j) // LANES * LANES
        shift = width * j - start
        layers = []
        for layer, value in enumerate(pair):
            amount = (layer * width - shift) % LANES
            window = value[:, start : start + LANES]
            layers.append(pltpu.roll(window, amount, 1) if amount else window)
        return jnp.where(lane < width, layers[0], layers[1])

    for j in range(length // width):
        out_ref[j, 0:ROWS] = block(dens, j)
        out_ref[j, ROWS : 2 * ROWS] = block(index, j)
        out_ref[j, 2 * ROWS : 3 * ROWS] = jnp.where(
            lane % width == 0, block(before, j), block(after, j)
        )


def edge_kernel(got_ref, low_ref, high_ref):
    low_ref[0] = got_ref[:, 0, :]
    low_ref[1] = got_ref[:, 2 * ROWS, :]
    high_ref[0] = got_ref[:, ROWS - 1, :]
    high_ref[1] = got_ref[:, 3 * ROWS - 1, :]


def edge_pick_kernel(got_ref, edge_ref):
    first = lax.axis_index("gx") == 0
    edge_ref[0] = jnp.where(first, got_ref[:, ROWS - 1, :], got_ref[:, 0, :])
    edge_ref[1] = jnp.where(first, got_ref[:, 3 * ROWS - 1, :], got_ref[:, 2 * ROWS, :])


def trade(value, lane, width):
    if 2 * width == LANES:
        return pltpu.roll(value, width, 1)
    return jnp.where(lane < width, pltpu.roll(value, LANES - width, 1), pltpu.roll(value, width, 1))


def gather_rows(parts, index):
    within = index & (LANES - 1)
    value = jnp.take_along_axis(parts[0], within, axis=1, mode="promise_in_bounds")
    for k in range(1, len(parts)):
        more = jnp.take_along_axis(parts[k], within, axis=1, mode="promise_in_bounds")
        value = jnp.where(index >= k * LANES, more, value)
    return value


def lighting(grad_z, grad_x, grad_y):
    inverse = lax.rsqrt(grad_z * grad_z + grad_x * grad_x + grad_y * grad_y + 1.0)
    ndl = (0.48 * grad_z + 0.6 * grad_x + 0.64 * grad_y) * inverse
    ndh = (0.86023 * grad_z + 0.34875 * grad_x + 0.372 * grad_y) * inverse
    shine = jnp.maximum(ndh, 0.0)
    shine = shine * shine
    shine = shine * shine
    shine = shine * shine
    return 0.3 + 0.6 * jnp.abs(ndl) + 0.4 * shine


def along_y(inner, outer, width):
    lane = lax.broadcasted_iota(jnp.int32, inner.shape, 1)
    before = jnp.where(lane % width == 0, outer, pltpu.roll(inner, 1, 1))
    after = jnp.where(lane % width == width - 1, outer, pltpu.roll(inner, LANES - 1, 1))
    return before, after


def render_kernel(width, step_len, got_ref, table_ref, image_ref, grad_ref, weight_ref):
    bricks = got_ref.shape[0]
    levels = table_ref.shape[1]
    lane = lax.broadcasted_iota(jnp.int32, (ROWS, LANES), 1)
    row = lax.broadcasted_iota(jnp.int32, (ROWS, LANES), 0)
    front_layer = lane < width
    zero = jnp.zeros((ROWS, LANES), jnp.float32)
    table = [
        [
            jnp.broadcast_to(table_ref[c : c + 1, start : start + LANES], (ROWS, LANES))
            for start in range(0, levels, LANES)
        ]
        for c in range(4)
    ]

    def with_ends(values):
        return [zero] + [trade(value, lane, width) for value in values] + [zero]

    dens = [got_ref[k, 0:ROWS] for k in range(bricks)]
    side = [got_ref[k, 2 * ROWS : 3 * ROWS] for k in range(bricks)]
    dens_other, side_other = with_ends(dens), with_ends(side)

    def stencil(value, other, k):
        behind = jnp.where(front_layer, other[k + 1], other[k + 2])
        ahead = jnp.where(front_layer, other[k], other[k + 1])
        planes = (behind - ahead, ahead + 2.0 * value + behind)
        below = [jnp.where(row == 0, 0.0, pltpu.roll(plane, 1, 0)) for plane in planes]
        above = [jnp.where(row == ROWS - 1, 0.0, pltpu.roll(plane, ROWS - 1, 0)) for plane in planes]
        return (
            below[0] + 2.0 * planes[0] + above[0],
            above[1] - below[1],
            below[1] + 2.0 * planes[1] + above[1],
        )

    front = jnp.ones((ROWS, LANES), jnp.float32)
    image = [zero, zero, zero]
    for k in range(bricks):
        inner = stencil(dens[k], dens_other, k)
        outer = stencil(side[k], side_other, k)
        before, after = along_y(inner[0], outer[0], width)
        grad_z = (before + 2.0 * inner[0] + after) * 0.5
        before, after = along_y(inner[1], outer[1], width)
        grad_x = (before + 2.0 * inner[1] + after) * 0.5
        before, after = along_y(inner[2], outer[2], width)
        grad_y = (after - before) * 0.5
        lit = lighting(grad_z, grad_x, grad_y)

        index = got_ref[k, ROWS : 2 * ROWS].astype(jnp.int32)
        alpha = 1.0 - jnp.exp(-gather_rows(table[3], index) * dens[k] * step_len)
        transmit = 1.0 - alpha
        transmit_other = trade(transmit, lane, width)
        seen = jnp.where(front_layer, front, front * transmit_other) * alpha
        front = front * (transmit * transmit_other)
        for part, grad in enumerate((grad_z, grad_x, grad_y)):
            grad_ref[part, k] = grad
        for c in range(3):
            weight = seen * gather_rows(table[c], index)
            weight_ref[c, k] = weight
            image[c] = image[c] + weight * lit

    for c in range(3):
        image_ref[c] = image[c] + trade(image[c], lane, width)
    image_ref[3] = 1.0 - front


def finish_kernel(width, paired, image_ref, grad_ref, weight_ref, *refs):
    edge_refs, out_ref = refs[:-1], refs[-1]
    bricks = grad_ref.shape[1]
    brick = lax.broadcasted_iota(jnp.int32, (bricks, LANES), 0)
    lane = lax.broadcasted_iota(jnp.int32, (bricks, LANES), 1)

    def planes(values):
        other = trade(values, lane, width)
        later = jnp.where(brick == bricks - 1, 0.0, pltpu.roll(other, bricks - 1, 0))
        earlier = jnp.where(brick == 0, 0.0, pltpu.roll(other, 1, 0))
        behind = jnp.where(lane < width, other, later)
        ahead = jnp.where(lane < width, earlier, other)
        return (behind - ahead, ahead + 2.0 * values + behind)

    def outermost(edge_ref, grads, weights, sign):
        delta, total = planes(edge_ref[0])
        delta_side, total_side = planes(edge_ref[1])
        before, after = along_y(delta, delta_side, width)
        grad_z = grads[0] + (before + 2.0 * delta + after) * 0.5
        before, after = along_y(total, total_side, width)
        grad_x = grads[1] + sign * ((before + 2.0 * total + after) * 0.5)
        grad_y = grads[2] + (after - before) * 0.5
        lit = lighting(grad_z, grad_x, grad_y)
        sums = [jnp.sum(weight * lit, axis=0, keepdims=True) for weight in weights]
        return [total + trade(total, lane[:1], width) for total in sums]

    def row_of(ref, row):
        return [ref[part, :, row, :] for part in range(3)]

    row = lax.broadcasted_iota(jnp.int32, (ROWS, width), 0)
    image = [image_ref[c][:, :width] for c in range(3)]
    if paired:
        first = lax.axis_index("gx") == 0
        pick = lambda ref: [
            jnp.where(first, high, low) for high, low in zip(row_of(ref, ROWS - 1), row_of(ref, 0))
        ]
        sign = jnp.where(first, 1.0, -1.0)
        done = outermost(edge_refs[0], pick(grad_ref), pick(weight_ref), sign)
        place = jnp.where(first, ROWS - 1, 0)
        for c in range(3):
            out_ref[c] = jnp.where(row == place, done[c][:, :width], image[c])
    else:
        low = outermost(edge_refs[0], row_of(grad_ref, 0), row_of(weight_ref, 0), -1.0)
        last = ROWS - 1
        high = outermost(edge_refs[1], row_of(grad_ref, last), row_of(weight_ref, last), 1.0)
        for c in range(3):
            value = jnp.where(row == 0, low[c][:, :width], image[c])
            out_ref[c] = jnp.where(row == last, high[c][:, :width], value)
    out_ref[3] = image_ref[3][:, :width]


def body(density, tf_index, tf_table):
    bricks, ranks = lax.axis_size("depth"), lax.axis_size("gx")
    layers, rows, length = density.shape
    width = length // bricks
    assert layers == 2 and rows == ROWS and 2 * width <= LANES and LANES % width == 0
    step_len = 1.0 / (layers * bricks)
    packed = pl.pallas_call(
        functools.partial(pack_kernel, width),
        out_shape=jax.ShapeDtypeStruct((bricks, BLOCK, LANES), jnp.float32),
        in_specs=[pl.BlockSpec(memory_space=pltpu.HBM)] * 2,
        out_specs=WHOLE,
        scratch_shapes=[
            pltpu.VMEM(density.shape, density.dtype),
            pltpu.VMEM(tf_index.shape, tf_index.dtype),
            pltpu.SemaphoreType.DMA,
            pltpu.SemaphoreType.DMA,
        ],
        name="pack", compiler_params=PARAMS,
    )(*(pltpu.with_memory_space_constraint(a, pltpu.HBM) for a in (density, tf_index)))
    got = lax.all_to_all(packed, "depth", 0, 0, tiled=True)
    edge = jax.ShapeDtypeStruct((2, bricks, LANES), jnp.float32)
    paired = ranks == 2
    if paired:
        mine = pl.pallas_call(
            edge_pick_kernel, out_shape=edge, in_specs=[WHOLE], out_specs=WHOLE, name="edge", compiler_params=PARAMS
        )(got)
        edges = [lax.ppermute(mine, "gx", [(0, 1), (1, 0)])]
    else:
        first, last = pl.pallas_call(
            edge_kernel, out_shape=[edge] * 2, in_specs=[WHOLE], out_specs=[WHOLE] * 2, name="edge", compiler_params=PARAMS
        )(got)
        edges = [
            lax.ppermute(last, "gx", [(i, i + 1) for i in range(ranks - 1)]),
            lax.ppermute(first, "gx", [(i + 1, i) for i in range(ranks - 1)]),
        ]
    voxels = jax.ShapeDtypeStruct((3, bricks, ROWS, LANES), jnp.float32)
    parts = pl.pallas_call(
        functools.partial(render_kernel, width, step_len),
        out_shape=[jax.ShapeDtypeStruct((4, ROWS, LANES), jnp.float32), voxels, voxels],
        in_specs=[WHOLE] * 2,
        out_specs=[WHOLE] * 3,
        cost_estimate=pl.CostEstimate(flops=1 << 24, bytes_accessed=1 << 23, transcendentals=0),
        name="render",
        compiler_params=PARAMS,
    )(got, tf_table)
    return pl.pallas_call(
        functools.partial(finish_kernel, width, paired),
        out_shape=jax.ShapeDtypeStruct((4, rows, width), jnp.float32),
        in_specs=[WHOLE] * (3 + len(edges)),
        out_specs=WHOLE,
        name="finish",
        compiler_params=PARAMS,
    )(*parts, *edges)


def solution(mesh):
    in_specs = (P("depth", "gx", None), P("depth", "gx", None), P())
    out_specs = P(None, "gx", "depth")
    return jax.shard_map(body, mesh=mesh, in_specs=in_specs, out_specs=out_specs, check_vma=False)
```

time: 23.1 us -> 22.1 us (0.957)
  waiting for transfers between devices: 2.22 us -> 0.97 us
  Pallas kernels: 2.95 us -> 3.22 us
    ppermute x1, waiting for transfers between devices: 2.22 us -> 0.97 us  [body(): edges = [lax.ppermute(mine, 'gx', [(0, 1), (1, 0)])]]
    pallas_call x1 -> x2, Pallas kernels: 1.83 us -> 2.1 us  [the longest x1 1.25 us: body(): pl.pallas_call(functools.partial(render_kernel, width, step_len), out_sha...]
  transfers between devices with their start and end apart: 1 -> 1, of which waited for: 1 -> 1; matrix products, arithmetic and copies ran while one was open for 0% -> 0% of each run, Pallas kernels for 0% -> 6%
where the time goes in v3:
time: 22.1 us; the launch traced here: 21.9 us
  blocking collectives  16.1 us (73%)
  Pallas kernels  3.22 us (15%)
  starting transfers between devices  1.58 us (7%)
  waiting for transfers between devices  0.97 us (4%)
    all_to_all x1, blocking collectives, body(): got = lax.all_to_all(packed, 'depth', 0, 0, tiled=True)  16.1 us
    ppermute x1, starting transfers between devices, body(): edges = [lax.ppermute(mine, 'gx', [(0, 1), (1, 0)])]  1.58 us
    pallas_call x1, Pallas kernels, body(): pl.pallas_call(functools.partial(render_kernel, width, step_len), out_sha...  1.25 us
    pallas_call x1, Pallas kernels, body(): pl.pallas_call(functools.partial(pack_kernel, width), out_shape=jax.Shape...  1.1 us
    ppermute x1, waiting for transfers between devices, body(): edges = [lax.ppermute(mine, 'gx', [(0, 1), (1, 0)])]  0.97 us
    pallas_call x1, Pallas kernels, body(): pl.pallas_call(functools.partial(finish_kernel, width, paired), out_shape...  0.86 us
  transfers between devices with their start and end apart: 1, of which 1 were waited for; matrix products, arithmetic and copies ran while one was open for 0% of the time, Pallas kernels for 6%

profile of v3, /device:TPU:0, one launch (start us, length us, event | category | flops | bytes accessed | tf_op | source)
XLA Modules:
  0.0 21.9 jit_solution(11349075061769927185)
XLA Ops:
  0.0 1.1 %pack.1 = f32[16,24,128]{2,1,0:T(8,128)S(1)} custom-call(f32[2,8,1024]{2,1,0:T(8,128)} %dens_hbm.1, s32[2,8,1024]{2,1,0:T(8,128)} %index_hbm.1), custom_call_target="tpu_custom_call" | custom-call | tf_op jit(solution)/shard_map/pack/pallas_call | solution.py:218
  1.1 16.1 %all_to_all.5.got_ref = f32[16,24,128]{2,1,0:T(8,128)S(1)} all-to-all(f32[16,24,128]{2,1,0:T(8,128)S(1)} %pack.1), channel_id=1, replica_groups=mesh['depth'=16,'gx'=2] {'depth'}, dimensions={0} | all-to-all | bytes 393216 | tf_op jit(solution)/shard_map/all_to_all | solution.py:231
  17.3 0.0 copy-start
  17.3 1.6 %collective-permute-start = (f32[2,16,128]{2,1,0:T(8,128)S(1)}, f32[2,16,128]{2,1,0:T(8,128)S(1)}, u32[]{:S(2)}, u32[]{:S(2)}) collective-permute-start(f32[2,16,128]{2,1,0:T(8,128)S(1)} %edge.1), channel_id=1, source_target_pairs={{0,1},{1,0},{2,3},{3,2},{4,5},{5,4},{6,7},{7,6},{8,9},{9,8},{10,11... | collective-permute-start | bytes 49160 | tf_op jit(solution)/shard_map/ppermute | solution.py:238
  18.9 0.0 copy-done
  18.9 1.2 %render.1 = (f32[4,8,128]{2,1,0:T(8,128)S(1)}, f32[3,16,8,128]{3,2,1,0:T(8,128)S(1)}, f32[3,16,8,128]{3,2,1,0:T(8,128)S(1)}) custom-call(f32[16,24,128]{2,1,0:T(8,128)S(1)} %all_to_all.5.got_ref, f32[4,256]{1,0:T(4,128)S(1)} %copy-done), custom_call_target="tpu_custom_call" | custom-call | flops 16777216 | bytes 8388608 | tf_op jit(solution)/shard_map/render/pallas_call | solution.py:248
  20.1 1.0 %collective-permute-done.refs_0_ = f32[2,16,128]{2,1,0:T(8,128)S(1)} collective-permute-done((f32[2,16,128]{2,1,0:T(8,128)S(1)}, f32[2,16,128]{2,1,0:T(8,128)S(1)}, u32[]{:S(2)}, u32[]{:S(2)}) %collective-permute-start) | collective-permute-done | bytes 16416 | tf_op jit(solution)/shard_map/ppermute | solution.py:238
  21.1 0.9 %finish.1 = f32[4,8,64]{2,1,0:T(8,128)} custom-call(f32[4,8,128]{2,1,0:T(8,128)S(1)} %get-tuple-element.8.image_ref, f32[3,16,8,128]{3,2,1,0:T(8,128)S(1)} %get-tuple-element.9.grad_ref, f32[3,16,8,128]{3,2,1,0:T(8,128)S(1)} %get-tuple-element.10.weight_ref, f32[2,16,128]{2,1,0:T(8,128)S(1)} %collective-permute-done.refs_0_), custom_call_target="tpu_custom_call" | custom-call | tf_op jit(solution)/shard_map/finish/pallas_call | solution.py:257
  (1 shorter events, 0.0 us)
Async XLA Ops:
  17.3 1.6 %copy-start = (f32[4,256]{1,0:T(4,128)S(1)}, f32[4,256]{1,0:T(4,128)}, u32[]{:S(2)}) copy-start(f32[4,256]{1,0:T(4,128)} %table_ref.1) | copy-start | bytes 12292
  17.3 3.8 %collective-permute-start = (f32[2,16,128]{2,1,0:T(8,128)S(1)}, f32[2,16,128]{2,1,0:T(8,128)S(1)}, u32[]{:S(2)}, u32[]{:S(2)}) collective-permute-start(f32[2,16,128]{2,1,0:T(8,128)S(1)} %edge.1), channel_id=1, source_target_pairs={{0,1},{1,0},{2,3},{3,2},{4,5},{5,4},{6,7},{7,6},{8,9},{9,8},{10,11... | collective-permute-start | bytes 49160 | tf_op jit(solution)/shard_map/ppermute | solution.py:238

commit v4 on v3

--- a/solution.py
+++ b/solution.py
@@ -10,6 +10,9 @@
 LANES = 128
 ROWS = 8
 BLOCK = 3 * ROWS
+INNER = 4
+FAR = (1, 2, 3, 0)
+NEAR = (-3, -2, -1, 0)
 WHOLE = pl.BlockSpec(memory_space=pltpu.VMEM)
 PARAMS = pltpu.CompilerParams(vmem_limit_bytes=4 << 20)
 
@@ -45,6 +48,128 @@
         out_ref[j, 2 * ROWS : 3 * ROWS] = jnp.where(
             lane % width == 0, block(before, j), block(after, j)
         )
+
+
+def goal(rank, step, count):
+    return (rank + step) % count if step >= 0 else rank ^ -step
+
+
+def origin(rank, step, count):
+    return (rank + count - step) % count if step >= 0 else rank ^ -step
+
+
+def first_kernel(inner, masks, dens_hbm, index_hbm, *refs):
+    outs, (dens_ref, index_ref, dens_sem, index_sem) = refs[:-4], refs[-4:]
+    groups = len(outs)
+    span = dens_ref.shape[2] // groups
+    tiles = span // LANES
+    dens_copy = pltpu.make_async_copy(dens_hbm, dens_ref, dens_sem)
+    index_copy = pltpu.make_async_copy(index_hbm, index_ref, index_sem)
+    dens_copy.start()
+    index_copy.start()
+    mine = lax.axis_index("depth") // inner
+    lane = lax.broadcasted_iota(jnp.int32, (ROWS, LANES), 1)
+    dens_copy.wait()
+    for mask, out_ref in zip(masks, outs):
+        group = goal(mine, mask, groups)
+        side = jnp.zeros((ROWS, LANES), jnp.float32)
+        for layer in range(2):
+            for tile in range(tiles):
+                start = pl.multiple_of(group * span + tile * LANES, LANES)
+                out_ref[layer * tiles + tile] = dens_ref[layer, :, pl.ds(start, LANES)]
+            before = pl.multiple_of(jnp.maximum(group * tiles - 1, 0) * LANES, LANES)
+            after = pl.multiple_of(jnp.minimum((group + 1) * tiles, groups * tiles - 1) * LANES, LANES)
+            left = pltpu.roll(dens_ref[layer, :, pl.ds(before, LANES)], 1 + layer, 1)
+            right = pltpu.roll(dens_ref[layer, :, pl.ds(after, LANES)], LANES - 1 - layer, 1)
+            side = jnp.where(lane == layer, jnp.where(group == 0, 0.0, left), side)
+            side = jnp.where(
+                lane == LANES - 1 - layer, jnp.where(group == groups - 1, 0.0, right), side
+            )
+        out_ref[4 * tiles] = side
+    index_copy.wait()
+    for mask, out_ref in zip(masks, outs):
+        group = goal(mine, mask, groups)
+        for layer in range(2):
+            for tile in range(tiles):
+                start = pl.multiple_of(group * span + tile * LANES, LANES)
+                value = index_ref[layer, :, pl.ds(start, LANES)]
+                out_ref[(2 + layer) * tiles + tile] = value.astype(jnp.float32)
+
+
+def second_kernel(width, inner, masks, *refs):
+    pieces, outs, scratch = refs[:inner], refs[inner:-1], refs[-1]
+    tiles = (pieces[0].shape[0] - 1) // 4
+    lane = lax.broadcasted_iota(jnp.int32, (ROWS, LANES), 1)
+    side = [jnp.zeros((ROWS, LANES), jnp.float32) for _ in range(inner)]
+    for m, piece in enumerate(pieces):
+        ends = piece[4 * tiles]
+        before, after = [], []
+        for layer in range(2):
+            value = [piece[layer * tiles + tile] for tile in range(tiles)]
+            down = [pltpu.roll(v, 1, 1) for v in value]
+            up = [pltpu.roll(v, LANES - 1, 1) for v in value]
+            left = pltpu.roll(ends, LANES - layer, 1) if layer else ends
+            right = pltpu.roll(ends, layer, 1) if layer else ends
+            before.append(
+                [jnp.where(lane == 0, d, e) for d, e in zip([left] + down[:-1], down)]
+            )
+            after.append(
+                [jnp.where(lane == LANES - 1, d, e) for d, e in zip(up[1:] + [right], up)]
+            )
+        dens = [[piece[layer * tiles + tile] for tile in range(tiles)] for layer in range(2)]
+        index = [[piece[(2 + layer) * tiles + tile] for tile in range(tiles)] for layer in range(2)]
+
+        def block(pair, t):
+            tile, shift = divmod(width * t, LANES)
+            layers = []
+            for layer, value in enumerate(pair):
+                amount = (layer * width - shift) % LANES
+                layers.append(pltpu.roll(value[tile], amount, 1) if amount else value[tile])
+            return jnp.where(lane < width, layers[0], layers[1])
+
+        for t in range(inner):
+            scratch[t, m] = block(dens, t)
+            scratch[t, inner + m] = block(index, t)
+            first, last = block(before, t), block(after, t)
+            first = pltpu.roll(first, m, 1) if m else first
+            last = pltpu.roll(last, LANES - m, 1) if m else last
+            side[t] = jnp.where(lane % width == m, first, side[t])
+            side[t] = jnp.where(lane % width == width - 1 - m, last, side[t])
+    for t in range(inner):
+        scratch[t, 2 * inner] = side[t]
+    mine = lax.axis_index("depth") % inner
+    for mask, out_ref in zip(masks, outs):
+        out_ref[...] = scratch[goal(mine, mask, inner)]
+
+
+def arrange_kernel(width, inner, far, near, paired, *refs):
+    pieces, (got_ref, edge_refs) = refs[:inner], (refs[inner], refs[inner + 1 :])
+    groups = (pieces[0].shape[0] - 1) // 2
+    mine = lax.axis_index("depth")
+    lane = lax.broadcasted_iota(jnp.int32, (ROWS, LANES), 1)
+    for n, piece in zip(near, pieces):
+        sides = piece[2 * groups]
+        for m in range(groups):
+            brick = origin(mine // inner, far[m], groups) * inner + origin(mine % inner, n, inner)
+            first = pltpu.roll(sides, LANES - m, 1) if m else sides
+            last = pltpu.roll(sides, m, 1) if m else sides
+            got_ref[brick, 0:ROWS] = piece[m]
+            got_ref[brick, ROWS : 2 * ROWS] = piece[groups + m]
+            got_ref[brick, 2 * ROWS : 3 * ROWS] = jnp.where(lane % width == 0, first, last)
+    if paired:
+        edge_pick_kernel(got_ref, *edge_refs)
+    else:
+        edge_kernel(got_ref, *edge_refs)
+
+
+def exchange(values, masks, scale):
+    count = lax.axis_size("depth")
+    arrived = []
+    for value, mask in zip(values, masks):
+        rank = lambda i: i // scale % INNER
+        pairs = [(i, i + (goal(rank(i), mask, INNER) - rank(i)) * scale) for i in range(count)]
+        arrived.append(lax.ppermute(value, "depth", pairs) if mask else value)
+    return arrived
 
 
 def edge_kernel(got_ref, low_ref, high_ref):
@@ -215,34 +340,73 @@
     width = length // bricks
     assert layers == 2 and rows == ROWS and 2 * width <= LANES and LANES % width == 0
     step_len = 1.0 / (layers * bricks)
-    packed = pl.pallas_call(
-        functools.partial(pack_kernel, width),
-        out_shape=jax.ShapeDtypeStruct((bricks, BLOCK, LANES), jnp.float32),
-        in_specs=[pl.BlockSpec(memory_space=pltpu.HBM)] * 2,
-        out_specs=WHOLE,
-        scratch_shapes=[
-            pltpu.VMEM(density.shape, density.dtype),
-            pltpu.VMEM(tf_index.shape, tf_index.dtype),
-            pltpu.SemaphoreType.DMA,
-            pltpu.SemaphoreType.DMA,
-        ],
-        name="pack", compiler_params=PARAMS,
-    )(*(pltpu.with_memory_space_constraint(a, pltpu.HBM) for a in (density, tf_index)))
-    got = lax.all_to_all(packed, "depth", 0, 0, tiled=True)
     edge = jax.ShapeDtypeStruct((2, bricks, LANES), jnp.float32)
     paired = ranks == 2
+    inputs = [pltpu.with_memory_space_constraint(a, pltpu.HBM) for a in (density, tf_index)]
+    landing = [
+        pltpu.VMEM(density.shape, density.dtype),
+        pltpu.VMEM(tf_index.shape, tf_index.dtype),
+        pltpu.SemaphoreType.DMA,
+        pltpu.SemaphoreType.DMA,
+    ]
+    staged = bricks == INNER * INNER and width * INNER % LANES == 0
+    if staged:
+        tiles = 4 * (width * INNER // LANES) + 1
+        sent = pl.pallas_call(
+            functools.partial(first_kernel, INNER, FAR),
+            out_shape=[jax.ShapeDtypeStruct((tiles, ROWS, LANES), jnp.float32)] * INNER,
+            in_specs=[pl.BlockSpec(memory_space=pltpu.HBM)] * 2,
+            out_specs=[WHOLE] * INNER,
+            scratch_shapes=landing,
+            name="first",
+            compiler_params=PARAMS,
+        )(*inputs)
+        pieces = exchange(sent, FAR, INNER)
+        tiles = 2 * INNER + 1
+        sent = pl.pallas_call(
+            functools.partial(second_kernel, width, INNER, NEAR),
+            out_shape=[jax.ShapeDtypeStruct((tiles, ROWS, LANES), jnp.float32)] * INNER,
+            in_specs=[WHOLE] * INNER,
+            out_specs=[WHOLE] * INNER,
+            scratch_shapes=[pltpu.VMEM((INNER, tiles, ROWS, LANES), jnp.float32)],
+            name="second",
+            compiler_params=PARAMS,
+        )(*pieces)
+        pieces = exchange(sent, NEAR, 1)
+        got, *outer = pl.pallas_call(
+            functools.partial(arrange_kernel, width, INNER, FAR, NEAR, paired),
+            out_shape=[jax.ShapeDtypeStruct((bricks, BLOCK, LANES), jnp.float32)]
+            + [edge] * (1 if paired else 2),
+            in_specs=[WHOLE] * INNER,
+            out_specs=[WHOLE] * (2 if paired else 3),
+            name="arrange",
+            compiler_params=PARAMS,
+        )(*pieces)
+    else:
+        packed = pl.pallas_call(
+            functools.partial(pack_kernel, width),
+            out_shape=jax.ShapeDtypeStruct((bricks, BLOCK, LANES), jnp.float32),
+            in_specs=[pl.BlockSpec(memory_space=pltpu.HBM)] * 2,
+            out_specs=WHOLE,
+            scratch_shapes=landing,
+            name="pack",
+            compiler_params=PARAMS,
+        )(*inputs)
+        got = lax.all_to_all(packed, "depth", 0, 0, tiled=True)
+        outer = pl.pallas_call(
+            edge_pick_kernel if paired else edge_kernel,
+            out_shape=[edge] * (1 if paired else 2),
+            in_specs=[WHOLE],
+            out_specs=[WHOLE] * (1 if paired else 2),
+            name="edge",
+            compiler_params=PARAMS,
+        )(got)
     if paired:
-        mine = pl.pallas_call(
-            edge_pick_kernel, out_shape=edge, in_specs=[WHOLE], out_specs=WHOLE, name="edge", compiler_params=PARAMS
-        )(got)
-        edges = [lax.ppermute(mine, "gx", [(0, 1), (1, 0)])]
+        edges = [lax.ppermute(outer[0], "gx", [(0, 1), (1, 0)])]
     else:
-        first, last = pl.pallas_call(
-            edge_kernel, out_shape=[edge] * 2, in_specs=[WHOLE], out_specs=[WHOLE] * 2, name="edge", compiler_params=PARAMS
-        )(got)
         edges = [
-            lax.ppermute(last, "gx", [(i, i + 1) for i in range(ranks - 1)]),
-            lax.ppermute(first, "gx", [(i + 1, i) for i in range(ranks - 1)]),
+            lax.ppermute(outer[1], "gx", [(i, i + 1) for i in range(ranks - 1)]),
+            lax.ppermute(outer[0], "gx", [(i + 1, i) for i in range(ranks - 1)]),
         ]
     voxels = jax.ShapeDtypeStruct((3, bricks, ROWS, LANES), jnp.float32)
     parts = pl.pallas_call(

time: 22.1 us -> 20.1 us (0.910)
  blocking collectives: 16.1 us -> 0 us
  starting transfers between devices: 1.58 us -> 10.5 us
  waiting for transfers between devices: 0.97 us -> 5.89 us
  Pallas kernels: 3.22 us -> 3.46 us
    all_to_all x1 -> x0, blocking collectives: 16.1 us -> none  [body(): got = lax.all_to_all(packed, 'depth', 0, 0, tiled=True)]
    ppermute x1 -> x7, starting transfers between devices: 1.58 us -> 10.5 us  [the longest x6 8.96 us: exchange(): arrived.append(lax.ppermute(value, 'depth', pairs) if mask else value)]
    ppermute x1 -> x7, waiting for transfers between devices: 0.97 us -> 5.89 us  [the longest x6 4.92 us: exchange(): arrived.append(lax.ppermute(value, 'depth', pairs) if mask else value)]
    pallas_call x2 -> x3, Pallas kernels: 1.12 us -> 1.35 us  [the longest x1 0.97 us: body(): pl.pallas_call(functools.partial(first_kernel, INNER, FAR), out_shape=[ja...]
  transfers between devices with their start and end apart: 1 -> 7, of which waited for: 1 -> 5; matrix products, arithmetic and copies ran while one was open for 0% -> 0% of each run, Pallas kernels for 6% -> 6%
where the time goes in v4:
time: 20.1 us; the launch traced here: 19.9 us
  starting transfers between devices  10.5 us (52%)
  waiting for transfers between devices  5.89 us (29%)
  Pallas kernels  3.46 us (17%)
    ppermute x6, starting transfers between devices, exchange(): arrived.append(lax.ppermute(value, 'depth', pairs) if mask else value)  8.96 us
    ppermute x6, waiting for transfers between devices, exchange(): arrived.append(lax.ppermute(value, 'depth', pairs) if mask else value)  4.92 us
    ppermute x1, starting transfers between devices, body(): edges = [lax.ppermute(outer[0], 'gx', [(0, 1), (1, 0)])]  1.58 us
    pallas_call x1, Pallas kernels, body(): pl.pallas_call(functools.partial(render_kernel, width, step_len), out_sha...  1.25 us
    pallas_call x1, Pallas kernels, body(): pl.pallas_call(functools.partial(first_kernel, INNER, FAR), out_shape=[ja...  0.97 us
    ppermute x1, waiting for transfers between devices, body(): edges = [lax.ppermute(outer[0], 'gx', [(0, 1), (1, 0)])]  0.97 us
    pallas_call x1, Pallas kernels, body(): pl.pallas_call(functools.partial(finish_kernel, width, paired), out_shape...  0.86 us
  transfers between devices with their start and end apart: 7, of which 5 were waited for; matrix products, arithmetic and copies ran while one was open for 0% of the time, Pallas kernels for 6%

profile of v4, /device:TPU:0, one launch (start us, length us, event | category | flops | bytes accessed | tf_op | source)
XLA Modules:
  0.0 19.9 jit_solution(3366935371667587348)
XLA Ops:
  0.0 1.0 %first.1 = (f32[9,8,128]{2,1,0:T(8,128)S(1)}, f32[9,8,128]{2,1,0:T(8,128)S(1)}, f32[9,8,128]{2,1,0:T(8,128)S(1)}, f32[9,8,128]{2,1,0:T(8,128)S(1)}) custom-call(f32[2,8,1024]{2,1,0:T(8,128)} %dens_hbm.1, s32[2,8,1024]{2,1,0:T(8,128)} %index_hbm.1), custom_call_target="tpu_custom_call" | custom-call | tf_op jit(solution)/shard_map/first/pallas_call | solution.py:355
  1.0 3.1 %collective-permute-start = (f32[9,8,128]{2,1,0:T(8,128)S(1)}, f32[9,8,128]{2,1,0:T(8,128)S(1)}, u32[]{:S(2)}, u32[]{:S(2)}) collective-permute-start(f32[9,8,128]{2,1,0:T(8,128)S(1)} %get-tuple-element.18), channel_id=1, source_target_pairs={{0,8},{2,10},{4,12},{6,14},{8,16},{10,18},{12,20},{14,22},{16,24},... | collective-permute-start | bytes 110600 | tf_op jit(solution)/shard_map/ppermute | solution.py:171
  4.1 2.6 %collective-permute-start.1 = (f32[9,8,128]{2,1,0:T(8,128)S(1)}, f32[9,8,128]{2,1,0:T(8,128)S(1)}, u32[]{:S(2)}, u32[]{:S(2)}) collective-permute-start(f32[9,8,128]{2,1,0:T(8,128)S(1)} %get-tuple-element.19), channel_id=1, source_target_pairs={{0,16},{2,18},{4,20},{6,22},{8,24},{10,26},{12,28},{14,30},{16,0},... | collective-permute-start | bytes 110600 | tf_op jit(solution)/shard_map/ppermute | solution.py:171
  6.7 1.3 %collective-permute-start.2 = (f32[9,8,128]{2,1,0:T(8,128)S(1)}, f32[9,8,128]{2,1,0:T(8,128)S(1)}, u32[]{:S(2)}, u32[]{:S(2)}) collective-permute-start(f32[9,8,128]{2,1,0:T(8,128)S(1)} %get-tuple-element.20), channel_id=1, source_target_pairs={{0,24},{2,26},{4,28},{6,30},{8,0},{10,2},{12,4},{14,6},{16,8},{18,... | collective-permute-start | bytes 110600 | tf_op jit(solution)/shard_map/ppermute | solution.py:171
  8.0 0.0 collective-permute-done.refs_0_
  8.0 1.3 %collective-permute-done.1.refs_1_ = f32[9,8,128]{2,1,0:T(8,128)S(1)} collective-permute-done((f32[9,8,128]{2,1,0:T(8,128)S(1)}, f32[9,8,128]{2,1,0:T(8,128)S(1)}, u32[]{:S(2)}, u32[]{:S(2)}) %collective-permute-start.1) | collective-permute-done | bytes 36896 | tf_op jit(solution)/shard_map/ppermute | solution.py:171
  9.3 1.3 %collective-permute-done.2.refs_2_ = f32[9,8,128]{2,1,0:T(8,128)S(1)} collective-permute-done((f32[9,8,128]{2,1,0:T(8,128)S(1)}, f32[9,8,128]{2,1,0:T(8,128)S(1)}, u32[]{:S(2)}, u32[]{:S(2)}) %collective-permute-start.2) | collective-permute-done | bytes 36896 | tf_op jit(solution)/shard_map/ppermute | solution.py:171
  10.6 0.3 %second.1 = (f32[9,8,128]{2,1,0:T(8,128)S(1)}, f32[9,8,128]{2,1,0:T(8,128)S(1)}, f32[9,8,128]{2,1,0:T(8,128)S(1)}, f32[9,8,128]{2,1,0:T(8,128)S(1)}) custom-call(f32[9,8,128]{2,1,0:T(8,128)S(1)} %collective-permute-done.refs_0_, f32[9,8,128]{2,1,0:T(8,128)S(1)} %collective-permute-done.1.refs_1_, f32[9,8,128]{2,1,0:T(8,128)S(1)} %collective-permute-done.2.refs_2_, ...), custom_call_target="tpu_custom_call" | custom-call | tf_op jit(solution)/shard_map/second/pallas_call | solution.py:366
  10.9 0.1 collective-permute-start.3
  11.0 1.6 %collective-permute-start.4 = (f32[9,8,128]{2,1,0:T(8,128)S(1)}, f32[9,8,128]{2,1,0:T(8,128)S(1)}, u32[]{:S(2)}, u32[]{:S(2)}) collective-permute-start(f32[9,8,128]{2,1,0:T(8,128)S(1)} %get-tuple-element.23), channel_id=1, source_target_pairs={{0,4},{2,6},{4,0},{6,2},{8,12},{10,14},{12,8},{14,10},{16,20},{18,... | collective-permute-start | bytes 110600 | tf_op jit(solution)/shard_map/ppermute | solution.py:171
  12.5 0.3 %collective-permute-start.5 = (f32[9,8,128]{2,1,0:T(8,128)S(1)}, f32[9,8,128]{2,1,0:T(8,128)S(1)}, u32[]{:S(2)}, u32[]{:S(2)}) collective-permute-start(f32[9,8,128]{2,1,0:T(8,128)S(1)} %get-tuple-element.24), channel_id=1, source_target_pairs={{0,2},{2,0},{4,6},{6,4},{8,10},{10,8},{12,14},{14,12},{16,18},{18,... | collective-permute-start | bytes 110600 | tf_op jit(solution)/shard_map/ppermute | solution.py:171
  12.8 1.9 %collective-permute-done.3.refs_0_ = f32[9,8,128]{2,1,0:T(8,128)S(1)} collective-permute-done((f32[9,8,128]{2,1,0:T(8,128)S(1)}, f32[9,8,128]{2,1,0:T(8,128)S(1)}, u32[]{:S(2)}, u32[]{:S(2)}) %collective-permute-start.3) | collective-permute-done | bytes 36896 | tf_op jit(solution)/shard_map/ppermute | solution.py:171
  14.7 0.4 %collective-permute-done.4.refs_1_ = f32[9,8,128]{2,1,0:T(8,128)S(1)} collective-permute-done((f32[9,8,128]{2,1,0:T(8,128)S(1)}, f32[9,8,128]{2,1,0:T(8,128)S(1)}, u32[]{:S(2)}, u32[]{:S(2)}) %collective-permute-start.4) | collective-permute-done | bytes 36896 | tf_op jit(solution)/shard_map/ppermute | solution.py:171
  15.1 0.0 collective-permute-done.5.refs_2_
  15.2 0.0 copy-start
  15.2 0.1 arrange.1
  15.3 1.6 %collective-permute-start.6 = (f32[2,16,128]{2,1,0:T(8,128)S(1)}, f32[2,16,128]{2,1,0:T(8,128)S(1)}, u32[]{:S(2)}, u32[]{:S(2)}) collective-permute-start(f32[2,16,128]{2,1,0:T(8,128)S(1)} %get-tuple-element.30), channel_id=1, source_target_pairs={{0,1},{1,0},{2,3},{3,2},{4,5},{5,4},{6,7},{7,6},{8,9},{9,8},{10,11... | collective-permute-start | bytes 49160 | tf_op jit(solution)/shard_map/ppermute | solution.py:405
  16.9 0.0 copy-done
  16.9 1.2 %render.1 = (f32[4,8,128]{2,1,0:T(8,128)S(1)}, f32[3,16,8,128]{3,2,1,0:T(8,128)S(1)}, f32[3,16,8,128]{3,2,1,0:T(8,128)S(1)}) custom-call(f32[16,24,128]{2,1,0:T(8,128)S(1)} %get-tuple-element.26.got_ref, f32[4,256]{1,0:T(4,128)S(1)} %copy-done), custom_call_target="tpu_custom_call" | custom-call | flops 16777216 | bytes 8388608 | tf_op jit(solution)/shard_map/render/pallas_call | solution.py:412
  18.1 1.0 %collective-permute-done.6.refs_0_ = f32[2,16,128]{2,1,0:T(8,128)S(1)} collective-permute-done((f32[2,16,128]{2,1,0:T(8,128)S(1)}, f32[2,16,128]{2,1,0:T(8,128)S(1)}, u32[]{:S(2)}, u32[]{:S(2)}) %collective-permute-start.6) | collective-permute-done | bytes 16416 | tf_op jit(solution)/shard_map/ppermute | solution.py:405
  19.1 0.9 %finish.1 = f32[4,8,64]{2,1,0:T(8,128)} custom-call(f32[4,8,128]{2,1,0:T(8,128)S(1)} %get-tuple-element.27.image_ref, f32[3,16,8,128]{3,2,1,0:T(8,128)S(1)} %get-tuple-element.28.grad_ref, f32[3,16,8,128]{3,2,1,0:T(8,128)S(1)} %get-tuple-element.29.weight_ref, f32[2,16,128]{2,1,0:T(8,128)S(1)} %collective-permute-done.6.refs_0_), custom_call_target="tpu_custom_call" | custom-call | tf_op jit(solution)/shard_map/finish/pallas_call | solution.py:421
Async XLA Ops:
  1.0 7.1 %collective-permute-start = (f32[9,8,128]{2,1,0:T(8,128)S(1)}, f32[9,8,128]{2,1,0:T(8,128)S(1)}, u32[]{:S(2)}, u32[]{:S(2)}) collective-permute-start(f32[9,8,128]{2,1,0:T(8,128)S(1)} %get-tuple-element.18), channel_id=1, source_target_pairs={{0,8},{2,10},{4,12},{6,14},{8,16},{10,18},{12,20},{14,22},{16,24},... | collective-permute-start | bytes 110600 | tf_op jit(solution)/shard_map/ppermute | solution.py:171
  4.1 5.2 %collective-permute-start.1 = (f32[9,8,128]{2,1,0:T(8,128)S(1)}, f32[9,8,128]{2,1,0:T(8,128)S(1)}, u32[]{:S(2)}, u32[]{:S(2)}) collective-permute-start(f32[9,8,128]{2,1,0:T(8,128)S(1)} %get-tuple-element.19), channel_id=1, source_target_pairs={{0,16},{2,18},{4,20},{6,22},{8,24},{10,26},{12,28},{14,30},{16,0},... | collective-permute-start | bytes 110600 | tf_op jit(solution)/shard_map/ppermute | solution.py:171
  6.7 4.0 %collective-permute-start.2 = (f32[9,8,128]{2,1,0:T(8,128)S(1)}, f32[9,8,128]{2,1,0:T(8,128)S(1)}, u32[]{:S(2)}, u32[]{:S(2)}) collective-permute-start(f32[9,8,128]{2,1,0:T(8,128)S(1)} %get-tuple-element.20), channel_id=1, source_target_pairs={{0,24},{2,26},{4,28},{6,30},{8,0},{10,2},{12,4},{14,6},{16,8},{18,... | collective-permute-start | bytes 110600 | tf_op jit(solution)/shard_map/ppermute | solution.py:171
  10.9 3.8 %collective-permute-start.3 = (f32[9,8,128]{2,1,0:T(8,128)S(1)}, f32[9,8,128]{2,1,0:T(8,128)S(1)}, u32[]{:S(2)}, u32[]{:S(2)}) collective-permute-start(f32[9,8,128]{2,1,0:T(8,128)S(1)} %get-tuple-element.22), channel_id=1, source_target_pairs={{0,6},{2,4},{4,2},{6,0},{8,14},{10,12},{12,10},{14,8},{16,22},{18,... | collective-permute-start | bytes 110600 | tf_op jit(solution)/shard_map/ppermute | solution.py:171
  11.0 4.2 %collective-permute-start.4 = (f32[9,8,128]{2,1,0:T(8,128)S(1)}, f32[9,8,128]{2,1,0:T(8,128)S(1)}, u32[]{:S(2)}, u32[]{:S(2)}) collective-permute-start(f32[9,8,128]{2,1,0:T(8,128)S(1)} %get-tuple-element.23), channel_id=1, source_target_pairs={{0,4},{2,6},{4,0},{6,2},{8,12},{10,14},{12,8},{14,10},{16,20},{18,... | collective-permute-start | bytes 110600 | tf_op jit(solution)/shard_map/ppermute | solution.py:171
  12.5 2.6 %collective-permute-start.5 = (f32[9,8,128]{2,1,0:T(8,128)S(1)}, f32[9,8,128]{2,1,0:T(8,128)S(1)}, u32[]{:S(2)}, u32[]{:S(2)}) collective-permute-start(f32[9,8,128]{2,1,0:T(8,128)S(1)} %get-tuple-element.24), channel_id=1, source_target_pairs={{0,2},{2,0},{4,6},{6,4},{8,10},{10,8},{12,14},{14,12},{16,18},{18,... | collective-permute-start | bytes 110600 | tf_op jit(solution)/shard_map/ppermute | solution.py:171
  15.2 1.7 %copy-start = (f32[4,256]{1,0:T(4,128)S(1)}, f32[4,256]{1,0:T(4,128)}, u32[]{:S(2)}) copy-start(f32[4,256]{1,0:T(4,128)} %table_ref.1) | copy-start | bytes 12292
  15.3 3.8 %collective-permute-start.6 = (f32[2,16,128]{2,1,0:T(8,128)S(1)}, f32[2,16,128]{2,1,0:T(8,128)S(1)}, u32[]{:S(2)}, u32[]{:S(2)}) collective-permute-start(f32[2,16,128]{2,1,0:T(8,128)S(1)} %get-tuple-element.30), channel_id=1, source_target_pairs={{0,1},{1,0},{2,3},{3,2},{4,5},{5,4},{6,7},{7,6},{8,9},{9,8},{10,11... | collective-permute-start | bytes 49160 | tf_op jit(solution)/shard_map/ppermute | solution.py:405

commit v5 on v3

--- a/solution.py
+++ b/solution.py
@@ -10,6 +10,7 @@
 LANES = 128
 ROWS = 8
 BLOCK = 3 * ROWS
+FAR = (1, 2, 3, 0)
 WHOLE = pl.BlockSpec(memory_space=pltpu.VMEM)
 PARAMS = pltpu.CompilerParams(vmem_limit_bytes=4 << 20)
 
@@ -45,6 +46,132 @@
         out_ref[j, 2 * ROWS : 3 * ROWS] = jnp.where(
             lane % width == 0, block(before, j), block(after, j)
         )
+
+
+def goal(rank, step, count):
+    return (rank + step) % count if step >= 0 else rank ^ -step
+
+
+def origin(rank, step, count):
+    return (rank + count - step) % count if step >= 0 else rank ^ -step
+
+
+def load_kernel(dens_hbm, index_hbm, dens_ref, index_ref, dens_sem, index_sem):
+    dens_copy = pltpu.make_async_copy(dens_hbm, dens_ref, dens_sem)
+    index_copy = pltpu.make_async_copy(index_hbm, index_ref, index_sem)
+    dens_copy.start()
+    index_copy.start()
+    dens_copy.wait()
+    index_copy.wait()
+
+
+def first_kernel(*refs):
+    own, other, outs, scratch = refs[0:2], refs[2:4], refs[4:-1], refs[-1]
+    half = LANES // 2
+    mine = lax.axis_index("depth")
+    core = mine % 2
+    lane = lax.broadcasted_iota(jnp.int32, (ROWS, LANES), 1)
+    zero = jnp.zeros((ROWS, LANES), jnp.float32)
+    tiles = own[0].shape[2] // LANES
+    sides = [zero] * (tiles // 2)
+
+    def tile_of(ref, layer, m):
+        return ref[layer, :, m * LANES : (m + 1) * LANES] if 0 <= m < tiles else zero
+
+    def pair(values):
+        first = pltpu.roll(values[0], half * core, 1)
+        return jnp.where(lane < half, first, pltpu.roll(values[1], half * (1 - core), 1))
+
+    for n, (dens_ref, index_ref) in enumerate((own, other)):
+        slot = core ^ n
+        for m in range(tiles):
+            group, place = divmod(m, 2)
+            scratch[group, 4 * place + slot] = pair([tile_of(dens_ref, layer, m) for layer in range(2)])
+            scratch[group, 4 * place + 2 + slot] = pair(
+                [tile_of(index_ref, layer, m).astype(jnp.float32) for layer in range(2)]
+            )
+            brick = 2 * place + slot
+            for layer in range(2):
+                here = tile_of(dens_ref, layer, m)
+                before = jnp.where(core == 0, tile_of(dens_ref, layer, m - 1), here)
+                after = jnp.where(core == 0, here, tile_of(dens_ref, layer, m + 1))
+                at = half * layer + brick
+                moved = pltpu.roll(before, (at + 1 + half * core) % LANES, 1)
+                sides[group] = jnp.where(lane == at, moved, sides[group])
+                at = half * layer + half - 1 - brick
+                moved = pltpu.roll(after, (at + half + half * core) % LANES, 1)
+                sides[group] = jnp.where(lane == at, moved, sides[group])
+    for group, side in enumerate(sides):
+        scratch[group, ROWS] = side
+    for step, out_ref in zip(FAR, outs):
+        out_ref[...] = scratch[goal(mine // 4, step, len(FAR))]
+
+
+def second_kernel(*refs):
+    pieces, (keep_ref, send_ref, near_ref, across_ref, scratch) = refs[: len(FAR)], refs[len(FAR) :]
+    half = LANES // 2
+    mine = lax.axis_index("depth")
+    place = mine // 2 % 2
+    lane = lax.broadcasted_iota(jnp.int32, (ROWS, LANES), 1)
+    for step, piece in zip(FAR, pieces):
+        group = origin(mine // 4, step, len(FAR))
+        packed = piece[ROWS]
+        for x in range(2):
+            for core in range(2):
+                brick = 2 * group + core
+                p = 2 * x + core
+                first = pltpu.roll(packed, LANES - p, 1) if p else packed
+                last = pltpu.roll(packed, p, 1) if p else packed
+                scratch[x, brick, 0:ROWS] = piece[4 * x + core]
+                scratch[x, brick, ROWS : 2 * ROWS] = piece[4 * x + 2 + core]
+                scratch[x, brick, 2 * ROWS :] = jnp.where(lane % half == 0, first, last)
+    bricks = scratch.shape[1]
+    sides = jnp.zeros((ROWS, LANES), jnp.float32)
+    for brick in range(bricks):
+        keep_ref[brick] = scratch[place, brick]
+        send_ref[brick] = scratch[1 - place, brick, 0:ROWS]
+        send_ref[bricks + brick] = scratch[1 - place, brick, ROWS : 2 * ROWS]
+        side = scratch[1 - place, brick, 2 * ROWS :]
+        first = pltpu.roll(side, brick, 1) if brick else side
+        last = pltpu.roll(side, LANES - brick, 1) if brick else side
+        sides = jnp.where(lane % half == brick, first, sides)
+        sides = jnp.where(lane % half == half - 1 - brick, last, sides)
+    send_ref[2 * bricks] = sides
+    top = lax.axis_index("gx") == 0
+    for ref, x in ((near_ref, place), (across_ref, 1 - place)):
+        for part in range(2):
+            low = 2 * ROWS * part
+            ref[part] = jnp.where(top, scratch[x, :, low + ROWS - 1, :], scratch[x, :, low, :])
+
+
+def staged_render_kernel(width, step_len, keep_ref, came_ref, table_ref, *refs):
+    outs, got_ref = refs[:-1], refs[-1]
+    half = LANES // 2
+    place = lax.axis_index("depth") // 2 % 2
+    lane = lax.broadcasted_iota(jnp.int32, (ROWS, LANES), 1)
+    bricks = keep_ref.shape[0]
+    packed = came_ref[2 * bricks]
+    for brick in range(bricks):
+        group, core = divmod(brick, 2)
+        got_ref[4 * group + 2 * place + core] = keep_ref[brick]
+        target = 4 * group + 2 * (1 - place) + core
+        first = pltpu.roll(packed, LANES - brick, 1) if brick else packed
+        last = pltpu.roll(packed, brick, 1) if brick else packed
+        got_ref[target, 0:ROWS] = came_ref[brick]
+        got_ref[target, ROWS : 2 * ROWS] = came_ref[bricks + brick]
+        got_ref[target, 2 * ROWS :] = jnp.where(lane % half == 0, first, last)
+    render_kernel(width, step_len, got_ref, table_ref, *outs)
+
+
+def staged_finish_kernel(width, image_ref, grad_ref, weight_ref, across_ref, near_ref, out_ref, edge_ref):
+    place = lax.axis_index("depth") // 2 % 2
+    for part in range(2):
+        near, across = near_ref[part], across_ref[part]
+        for x, value in enumerate((jnp.where(place == 0, near, across), jnp.where(place == 0, across, near))):
+            for group in range(len(FAR)):
+                start = 4 * group + 2 * x
+                edge_ref[part, start : start + 2] = value[2 * group : 2 * group + 2]
+    finish_kernel(width, True, image_ref, grad_ref, weight_ref, edge_ref, out_ref)
 
 
 def edge_kernel(got_ref, low_ref, high_ref):
@@ -209,40 +336,125 @@
     out_ref[3] = image_ref[3][:, :width]
 
 
+def staged_body(density, tf_index, tf_table):
+    bricks, groups = lax.axis_size("depth"), len(FAR)
+    layers, rows, length = density.shape
+    width = length // bricks
+    step_len = 1.0 / (layers * bricks)
+    half = bricks // 2
+
+    def call(kernel, out_shape, operands, name, scratch=(), cost=None, spec=WHOLE):
+        return pl.pallas_call(
+            kernel,
+            out_shape=out_shape,
+            in_specs=[spec] * len(operands),
+            out_specs=jax.tree.map(lambda _: WHOLE, out_shape),
+            scratch_shapes=scratch,
+            cost_estimate=cost,
+            name=name,
+            compiler_params=PARAMS,
+        )(*operands)
+
+    def block(*shape):
+        return jax.ShapeDtypeStruct(shape + (ROWS, LANES), jnp.float32)
+
+    def swap(value, mask):
+        return lax.ppermute(value, "depth", [(i, i ^ mask) for i in range(bricks)])
+
+    inputs = [pltpu.with_memory_space_constraint(a, pltpu.HBM) for a in (density, tf_index)]
+    theirs = [swap(value, 1) for value in (density, tf_index)]
+    ours = call(
+        load_kernel,
+        [jax.ShapeDtypeStruct(a.shape, a.dtype) for a in inputs],
+        inputs,
+        "load",
+        [pltpu.SemaphoreType.DMA] * 2,
+        pl.CostEstimate(flops=1 << 20, bytes_accessed=1 << 21, transcendentals=0),
+        pl.BlockSpec(memory_space=pltpu.HBM),
+    )
+    sent = call(
+        first_kernel,
+        [block(ROWS + 1)] * groups,
+        [*ours, *theirs],
+        "first",
+        [pltpu.VMEM((groups, ROWS + 1, ROWS, LANES), jnp.float32)],
+    )
+    came = []
+    for value, step in zip(sent, FAR):
+        pairs = [(i, goal(i // 4, step, groups) * 4 + i % 4) for i in range(bricks)]
+        came.append(lax.ppermute(value, "depth", pairs) if step else value)
+    edge = jax.ShapeDtypeStruct((2, half, LANES), jnp.float32)
+    keep, send, near, across = call(
+        second_kernel,
+        [jax.ShapeDtypeStruct((half, BLOCK, LANES), jnp.float32), block(2 * half + 1), edge, edge],
+        came,
+        "second",
+        [pltpu.VMEM((2, half, BLOCK, LANES), jnp.float32)],
+    )
+    other = swap(send, 2)
+    near = lax.ppermute(near, "gx", [(0, 1), (1, 0)])
+    across = lax.ppermute(
+        across, ("depth", "gx"), [(2 * i + g, 2 * (i ^ 2) + 1 - g) for i in range(bricks) for g in range(2)]
+    )
+    voxels = block(3, bricks)
+    parts = call(
+        functools.partial(staged_render_kernel, width, step_len),
+        [block(4), voxels, voxels],
+        [keep, other, tf_table],
+        "render",
+        [pltpu.VMEM((bricks, BLOCK, LANES), jnp.float32)],
+        pl.CostEstimate(flops=1 << 24, bytes_accessed=1 << 23, transcendentals=0),
+    )
+    return call(
+        functools.partial(staged_finish_kernel, width),
+        jax.ShapeDtypeStruct((4, rows, width), jnp.float32),
+        [*parts, across, near],
+        "finish",
+        [pltpu.VMEM((2, bricks, LANES), jnp.float32)],
+    )
+
+
 def body(density, tf_index, tf_table):
     bricks, ranks = lax.axis_size("depth"), lax.axis_size("gx")
     layers, rows, length = density.shape
     width = length // bricks
+    if bricks == 16 and ranks == 2 and layers == 2 and rows == ROWS and 2 * width == LANES:
+        return staged_body(density, tf_index, tf_table)
     assert layers == 2 and rows == ROWS and 2 * width <= LANES and LANES % width == 0
     step_len = 1.0 / (layers * bricks)
+    edge = jax.ShapeDtypeStruct((2, bricks, LANES), jnp.float32)
+    paired = ranks == 2
+    inputs = [pltpu.with_memory_space_constraint(a, pltpu.HBM) for a in (density, tf_index)]
+    landing = [
+        pltpu.VMEM(density.shape, density.dtype),
+        pltpu.VMEM(tf_index.shape, tf_index.dtype),
+        pltpu.SemaphoreType.DMA,
+        pltpu.SemaphoreType.DMA,
+    ]
     packed = pl.pallas_call(
         functools.partial(pack_kernel, width),
         out_shape=jax.ShapeDtypeStruct((bricks, BLOCK, LANES), jnp.float32),
         in_specs=[pl.BlockSpec(memory_space=pltpu.HBM)] * 2,
         out_specs=WHOLE,
-        scratch_shapes=[
-            pltpu.VMEM(density.shape, density.dtype),
-            pltpu.VMEM(tf_index.shape, tf_index.dtype),
-            pltpu.SemaphoreType.DMA,
-            pltpu.SemaphoreType.DMA,
-        ],
-        name="pack", compiler_params=PARAMS,
-    )(*(pltpu.with_memory_space_constraint(a, pltpu.HBM) for a in (density, tf_index)))
+        scratch_shapes=landing,
+        name="pack",
+        compiler_params=PARAMS,
+    )(*inputs)
     got = lax.all_to_all(packed, "depth", 0, 0, tiled=True)
-    edge = jax.ShapeDtypeStruct((2, bricks, LANES), jnp.float32)
-    paired = ranks == 2
+    outer = pl.pallas_call(
+        edge_pick_kernel if paired else edge_kernel,
+        out_shape=[edge] * (1 if paired else 2),
+        in_specs=[WHOLE],
+        out_specs=[WHOLE] * (1 if paired else 2),
+        name="edge",
+        compiler_params=PARAMS,
+    )(got)
     if paired:
-        mine = pl.pallas_call(
-            edge_pick_kernel, out_shape=edge, in_specs=[WHOLE], out_specs=WHOLE, name="edge", compiler_params=PARAMS
-        )(got)
-        edges = [lax.ppermute(mine, "gx", [(0, 1), (1, 0)])]
+        edges = [lax.ppermute(outer[0], "gx", [(0, 1), (1, 0)])]
     else:
-        first, last = pl.pallas_call(
-            edge_kernel, out_shape=[edge] * 2, in_specs=[WHOLE], out_specs=[WHOLE] * 2, name="edge", compiler_params=PARAMS
-        )(got)
         edges = [
-            lax.ppermute(last, "gx", [(i, i + 1) for i in range(ranks - 1)]),
-            lax.ppermute(first, "gx", [(i + 1, i) for i in range(ranks - 1)]),
+            lax.ppermute(outer[1], "gx", [(i, i + 1) for i in range(ranks - 1)]),
+            lax.ppermute(outer[0], "gx", [(i + 1, i) for i in range(ranks - 1)]),
         ]
     voxels = jax.ShapeDtypeStruct((3, bricks, ROWS, LANES), jnp.float32)
     parts = pl.pallas_call(

time: 22.1 us -> 19.4 us (0.88)
  blocking collectives: 16.1 us -> 0 us
  starting transfers between devices: 1.58 us -> 10.8 us
  waiting for transfers between devices: 0.97 us -> 5.1 us
    all_to_all x1 -> x0, blocking collectives: 16.1 us -> none  [body(): got = lax.all_to_all(packed, 'depth', 0, 0, tiled=True)]
    ppermute x1 -> x8, starting transfers between devices: 1.58 us -> 10.8 us  [the longest x3 6.7 us: staged_body(): came.append(lax.ppermute(value, 'depth', pairs) if step else value)]
    ppermute x1 -> x8, waiting for transfers between devices: 0.97 us -> 5.1 us  [the longest x3 2.61 us: staged_body(): came.append(lax.ppermute(value, 'depth', pairs) if step else value)]
    pallas_call x4 -> x5, Pallas kernels: 3.22 us -> 3.38 us  [call(): pl.pallas_call(kernel, out_shape=out_shape, in_specs=[spec] * len(operand...]
  transfers between devices with their start and end apart: 1 -> 8, of which waited for: 1 -> 8; matrix products, arithmetic and copies ran while one was open for 0% -> 0% of each run, Pallas kernels for 6% -> 11%
where the time goes in v5:
time: 19.4 us; the launch traced here: 19.3 us
  starting transfers between devices  10.8 us (56%)
  waiting for transfers between devices  5.1 us (26%)
  Pallas kernels  3.38 us (17%)
    ppermute x3, starting transfers between devices, staged_body(): came.append(lax.ppermute(value, 'depth', pairs) if step else value)  6.7 us
    pallas_call x5, Pallas kernels, call(): pl.pallas_call(kernel, out_shape=out_shape, in_specs=[spec] * len(operand...  3.38 us
    ppermute x3, waiting for transfers between devices, staged_body(): came.append(lax.ppermute(value, 'depth', pairs) if step else value)  2.61 us
    ppermute x3, starting transfers between devices, swap(): return lax.ppermute(value, 'depth', [(i, i ^ mask) for i in range(bricks)])  2.06 us
    ppermute x1, starting transfers between devices, staged_body(): lax.ppermute(across, ('depth', 'gx'), [(2 * i + g, 2 * (i ^ 2) + 1 - g) f...  1.49 us
    ppermute x3, waiting for transfers between devices, swap(): return lax.ppermute(value, 'depth', [(i, i ^ mask) for i in range(bricks)])  1.46 us
    ppermute x1, waiting for transfers between devices, staged_body(): near = lax.ppermute(near, 'gx', [(0, 1), (1, 0)])  0.6 us
    ppermute x1, starting transfers between devices, staged_body(): near = lax.ppermute(near, 'gx', [(0, 1), (1, 0)])  0.51 us
  transfers between devices with their start and end apart: 8, of which 8 were waited for; matrix products, arithmetic and copies ran while one was open for 0% of the time, Pallas kernels for 11%

profile of v5, /device:TPU:0, one launch (start us, length us, event | category | flops | bytes accessed | tf_op | source)
XLA Modules:
  0.0 19.3 jit_solution(18320176012938556056)
XLA Ops:
  0.0 0.5 %collective-permute-start = (f32[2,8,1024]{2,1,0:T(8,128)}, f32[2,8,1024]{2,1,0:T(8,128)S(1)}, u32[]{:S(2)}, u32[]{:S(2)}) collective-permute-start(f32[2,8,1024]{2,1,0:T(8,128)} %dens_hbm.1), channel_id=1, source_target_pairs={{0,2},{2,0},{4,6},{6,4},{8,10},{10,8},{12,14},{14,12},{16,18},{18,... | collective-permute-start | bytes 196616 | tf_op jit(solution)/shard_map/ppermute | solution.py:362
  0.5 0.0 collective-permute-start.1
  0.5 0.9 %load.1 = (f32[2,8,1024]{2,1,0:T(8,128)S(1)}, s32[2,8,1024]{2,1,0:T(8,128)S(1)}) custom-call(f32[2,8,1024]{2,1,0:T(8,128)} %dens_hbm.1, s32[2,8,1024]{2,1,0:T(8,128)} %index_hbm.1), custom_call_target="tpu_custom_call" | custom-call | flops 1048576 | bytes 2097152 | tf_op jit(solution)/shard_map/load/pallas_call | solution.py:347
  1.4 0.2 %collective-permute-done.refs_2_ = f32[2,8,1024]{2,1,0:T(8,128)S(1)} collective-permute-done((f32[2,8,1024]{2,1,0:T(8,128)}, f32[2,8,1024]{2,1,0:T(8,128)S(1)}, u32[]{:S(2)}, u32[]{:S(2)}) %collective-permute-start) | collective-permute-done | bytes 65568 | tf_op jit(solution)/shard_map/ppermute | solution.py:362
  1.6 0.4 %collective-permute-done.1.refs_3_ = s32[2,8,1024]{2,1,0:T(8,128)S(1)} collective-permute-done((s32[2,8,1024]{2,1,0:T(8,128)}, s32[2,8,1024]{2,1,0:T(8,128)S(1)}, u32[]{:S(2)}, u32[]{:S(2)}) %collective-permute-start.1) | collective-permute-done | bytes 65568 | tf_op jit(solution)/shard_map/ppermute | solution.py:362
  2.0 0.2 %first.1 = (f32[9,8,128]{2,1,0:T(8,128)S(1)}, f32[9,8,128]{2,1,0:T(8,128)S(1)}, f32[9,8,128]{2,1,0:T(8,128)S(1)}, f32[9,8,128]{2,1,0:T(8,128)S(1)}) custom-call(f32[2,8,1024]{2,1,0:T(8,128)S(1)} %get-tuple-element.18.refs_0_, s32[2,8,1024]{2,1,0:T(8,128)S(1)} %get-tuple-element.19.refs_1_, f32[2,8,1024]{2,1,0:T(8,128)S(1)} %collective-permute-done.refs_2_, ...), custom_call_target="tpu_custom_call" | custom-call | tf_op jit(solution)/shard_map/first/pallas_call | solution.py:347
  2.2 2.8 %collective-permute-start.2 = (f32[9,8,128]{2,1,0:T(8,128)S(1)}, f32[9,8,128]{2,1,0:T(8,128)S(1)}, u32[]{:S(2)}, u32[]{:S(2)}) collective-permute-start(f32[9,8,128]{2,1,0:T(8,128)S(1)} %get-tuple-element.20), channel_id=1, source_target_pairs={{0,8},{2,10},{4,12},{6,14},{8,16},{10,18},{12,20},{14,22},{16,24},... | collective-permute-start | bytes 110600 | tf_op jit(solution)/shard_map/ppermute | solution.py:385
  5.0 2.6 %collective-permute-start.3 = (f32[9,8,128]{2,1,0:T(8,128)S(1)}, f32[9,8,128]{2,1,0:T(8,128)S(1)}, u32[]{:S(2)}, u32[]{:S(2)}) collective-permute-start(f32[9,8,128]{2,1,0:T(8,128)S(1)} %get-tuple-element.21), channel_id=1, source_target_pairs={{0,16},{2,18},{4,20},{6,22},{8,24},{10,26},{12,28},{14,30},{16,0},... | collective-permute-start | bytes 110600 | tf_op jit(solution)/shard_map/ppermute | solution.py:385
  7.5 1.3 %collective-permute-start.4 = (f32[9,8,128]{2,1,0:T(8,128)S(1)}, f32[9,8,128]{2,1,0:T(8,128)S(1)}, u32[]{:S(2)}, u32[]{:S(2)}) collective-permute-start(f32[9,8,128]{2,1,0:T(8,128)S(1)} %get-tuple-element.22), channel_id=1, source_target_pairs={{0,24},{2,26},{4,28},{6,30},{8,0},{10,2},{12,4},{14,6},{16,8},{18,... | collective-permute-start | bytes 110600 | tf_op jit(solution)/shard_map/ppermute | solution.py:385
  8.9 0.1 collective-permute-done.2.refs_0_
  9.0 1.4 %collective-permute-done.3.refs_1_ = f32[9,8,128]{2,1,0:T(8,128)S(1)} collective-permute-done((f32[9,8,128]{2,1,0:T(8,128)S(1)}, f32[9,8,128]{2,1,0:T(8,128)S(1)}, u32[]{:S(2)}, u32[]{:S(2)}) %collective-permute-start.3) | collective-permute-done | bytes 36896 | tf_op jit(solution)/shard_map/ppermute | solution.py:385
  10.4 1.1 %collective-permute-done.4.refs_2_ = f32[9,8,128]{2,1,0:T(8,128)S(1)} collective-permute-done((f32[9,8,128]{2,1,0:T(8,128)S(1)}, f32[9,8,128]{2,1,0:T(8,128)S(1)}, u32[]{:S(2)}, u32[]{:S(2)}) %collective-permute-start.4) | collective-permute-done | bytes 36896 | tf_op jit(solution)/shard_map/ppermute | solution.py:385
  11.5 0.2 %second.1 = (f32[8,24,128]{2,1,0:T(8,128)S(1)}, f32[17,8,128]{2,1,0:T(8,128)S(1)}, f32[2,8,128]{2,1,0:T(8,128)S(1)}, f32[2,8,128]{2,1,0:T(8,128)S(1)}) custom-call(f32[9,8,128]{2,1,0:T(8,128)S(1)} %collective-permute-done.2.refs_0_, f32[9,8,128]{2,1,0:T(8,128)S(1)} %collective-permute-done.3.refs_1_, f32[9,8,128]{2,1,0:T(8,128)S(1)} %collective-permute-done.4.refs_2_, ...), custom_call_target="tpu_custom_call" | custom-call | tf_op jit(solution)/shard_map/second/pallas_call | solution.py:347
  11.7 0.0 copy-start
  11.7 1.6 %collective-permute-start.5 = (f32[17,8,128]{2,1,0:T(8,128)S(1)}, f32[17,8,128]{2,1,0:T(8,128)S(1)}, u32[]{:S(2)}, u32[]{:S(2)}) collective-permute-start(f32[17,8,128]{2,1,0:T(8,128)S(1)} %get-tuple-element.25), channel_id=1, source_target_pairs={{0,4},{2,6},{4,0},{6,2},{8,12},{10,14},{12,8},{14,10},{16,20},{18,... | collective-permute-start | bytes 208904 | tf_op jit(solution)/shard_map/ppermute | solution.py:362
  13.3 1.5 %collective-permute-start.6 = (f32[2,8,128]{2,1,0:T(8,128)S(1)}, f32[2,8,128]{2,1,0:T(8,128)S(1)}, u32[]{:S(2)}, u32[]{:S(2)}) collective-permute-start(f32[2,8,128]{2,1,0:T(8,128)S(1)} %get-tuple-element.29), channel_id=1, source_target_pairs={{0,5},{1,4},{2,7},{3,6},{4,1},{5,0},{6,3},{7,2},{8,13},{9,12},{10,... | collective-permute-start | bytes 24584 | tf_op jit(solution)/shard_map/ppermute | solution.py:396
  14.8 0.5 %collective-permute-start.7 = (f32[2,8,128]{2,1,0:T(8,128)S(1)}, f32[2,8,128]{2,1,0:T(8,128)S(1)}, u32[]{:S(2)}, u32[]{:S(2)}) collective-permute-start(f32[2,8,128]{2,1,0:T(8,128)S(1)} %get-tuple-element.30), channel_id=1, source_target_pairs={{0,1},{1,0},{2,3},{3,2},{4,5},{5,4},{6,7},{7,6},{8,9},{9,8},{10,11... | collective-permute-start | bytes 24584 | tf_op jit(solution)/shard_map/ppermute | solution.py:395
  15.3 0.9 %collective-permute-done.5.came_ref = f32[17,8,128]{2,1,0:T(8,128)S(1)} collective-permute-done((f32[17,8,128]{2,1,0:T(8,128)S(1)}, f32[17,8,128]{2,1,0:T(8,128)S(1)}, u32[]{:S(2)}, u32[]{:S(2)}) %collective-permute-start.5) | collective-permute-done | bytes 69664 | tf_op jit(solution)/shard_map/ppermute | solution.py:362
  16.2 0.0 copy-done
  16.2 1.2 %render.1 = (f32[4,8,128]{2,1,0:T(8,128)S(1)}, f32[3,16,8,128]{3,2,1,0:T(8,128)S(1)}, f32[3,16,8,128]{3,2,1,0:T(8,128)S(1)}) custom-call(f32[8,24,128]{2,1,0:T(8,128)S(1)} %get-tuple-element.24.keep_ref, f32[17,8,128]{2,1,0:T(8,128)S(1)} %collective-permute-done.5.came_ref, f32[4,256]{1,0:T(4,128)S(1)} %copy-done), custom_call_target="tpu_custom_call" | custom-call | flops 16777216 | bytes 8388608 | tf_op jit(solution)/shard_map/render/pallas_call | solution.py:347
  17.4 0.4 %collective-permute-done.6.across_ref = f32[2,8,128]{2,1,0:T(8,128)S(1)} collective-permute-done((f32[2,8,128]{2,1,0:T(8,128)S(1)}, f32[2,8,128]{2,1,0:T(8,128)S(1)}, u32[]{:S(2)}, u32[]{:S(2)}) %collective-permute-start.6) | collective-permute-done | bytes 8224 | tf_op jit(solution)/shard_map/ppermute | solution.py:396
  17.8 0.6 %collective-permute-done.7.near_ref = f32[2,8,128]{2,1,0:T(8,128)S(1)} collective-permute-done((f32[2,8,128]{2,1,0:T(8,128)S(1)}, f32[2,8,128]{2,1,0:T(8,128)S(1)}, u32[]{:S(2)}, u32[]{:S(2)}) %collective-permute-start.7) | collective-permute-done | bytes 8224 | tf_op jit(solution)/shard_map/ppermute | solution.py:395
  18.4 0.9 %finish.1 = f32[4,8,64]{2,1,0:T(8,128)} custom-call(f32[4,8,128]{2,1,0:T(8,128)S(1)} %get-tuple-element.26.image_ref, f32[3,16,8,128]{3,2,1,0:T(8,128)S(1)} %get-tuple-element.27.grad_ref, f32[3,16,8,128]{3,2,1,0:T(8,128)S(1)} %get-tuple-element.28.weight_ref, f32[2,8,128]{2,1,0:T(8,128)S(1)} %collective-permute-done.6.across_ref, ...), custom_call_target="tpu_custom_call" | custom-call | tf_op jit(solution)/shard_map/finish/pallas_call | solution.py:347
Async XLA Ops:
  0.0 1.6 %collective-permute-start = (f32[2,8,1024]{2,1,0:T(8,128)}, f32[2,8,1024]{2,1,0:T(8,128)S(1)}, u32[]{:S(2)}, u32[]{:S(2)}) collective-permute-start(f32[2,8,1024]{2,1,0:T(8,128)} %dens_hbm.1), channel_id=1, source_target_pairs={{0,2},{2,0},{4,6},{6,4},{8,10},{10,8},{12,14},{14,12},{16,18},{18,... | collective-permute-start | bytes 196616 | tf_op jit(solution)/shard_map/ppermute | solution.py:362
  0.5 1.5 %collective-permute-start.1 = (s32[2,8,1024]{2,1,0:T(8,128)}, s32[2,8,1024]{2,1,0:T(8,128)S(1)}, u32[]{:S(2)}, u32[]{:S(2)}) collective-permute-start(s32[2,8,1024]{2,1,0:T(8,128)} %index_hbm.1), channel_id=1, source_target_pairs={{0,2},{2,0},{4,6},{6,4},{8,10},{10,8},{12,14},{14,12},{16,18},{18,... | collective-permute-start | bytes 196616 | tf_op jit(solution)/shard_map/ppermute | solution.py:362
  2.2 6.8 %collective-permute-start.2 = (f32[9,8,128]{2,1,0:T(8,128)S(1)}, f32[9,8,128]{2,1,0:T(8,128)S(1)}, u32[]{:S(2)}, u32[]{:S(2)}) collective-permute-start(f32[9,8,128]{2,1,0:T(8,128)S(1)} %get-tuple-element.20), channel_id=1, source_target_pairs={{0,8},{2,10},{4,12},{6,14},{8,16},{10,18},{12,20},{14,22},{16,24},... | collective-permute-start | bytes 110600 | tf_op jit(solution)/shard_map/ppermute | solution.py:385
  5.0 5.4 %collective-permute-start.3 = (f32[9,8,128]{2,1,0:T(8,128)S(1)}, f32[9,8,128]{2,1,0:T(8,128)S(1)}, u32[]{:S(2)}, u32[]{:S(2)}) collective-permute-start(f32[9,8,128]{2,1,0:T(8,128)S(1)} %get-tuple-element.21), channel_id=1, source_target_pairs={{0,16},{2,18},{4,20},{6,22},{8,24},{10,26},{12,28},{14,30},{16,0},... | collective-permute-start | bytes 110600 | tf_op jit(solution)/shard_map/ppermute | solution.py:385
  7.5 4.0 %collective-permute-start.4 = (f32[9,8,128]{2,1,0:T(8,128)S(1)}, f32[9,8,128]{2,1,0:T(8,128)S(1)}, u32[]{:S(2)}, u32[]{:S(2)}) collective-permute-start(f32[9,8,128]{2,1,0:T(8,128)S(1)} %get-tuple-element.22), channel_id=1, source_target_pairs={{0,24},{2,26},{4,28},{6,30},{8,0},{10,2},{12,4},{14,6},{16,8},{18,... | collective-permute-start | bytes 110600 | tf_op jit(solution)/shard_map/ppermute | solution.py:385
  11.7 4.5 %copy-start = (f32[4,256]{1,0:T(4,128)S(1)}, f32[4,256]{1,0:T(4,128)}, u32[]{:S(2)}) copy-start(f32[4,256]{1,0:T(4,128)} %table_ref.1) | copy-start | bytes 12292
  11.7 4.5 %collective-permute-start.5 = (f32[17,8,128]{2,1,0:T(8,128)S(1)}, f32[17,8,128]{2,1,0:T(8,128)S(1)}, u32[]{:S(2)}, u32[]{:S(2)}) collective-permute-start(f32[17,8,128]{2,1,0:T(8,128)S(1)} %get-tuple-element.25), channel_id=1, source_target_pairs={{0,4},{2,6},{4,0},{6,2},{8,12},{10,14},{12,8},{14,10},{16,20},{18,... | collective-permute-start | bytes 208904 | tf_op jit(solution)/shard_map/ppermute | solution.py:362
  13.3 4.5 %collective-permute-start.6 = (f32[2,8,128]{2,1,0:T(8,128)S(1)}, f32[2,8,128]{2,1,0:T(8,128)S(1)}, u32[]{:S(2)}, u32[]{:S(2)}) collective-permute-start(f32[2,8,128]{2,1,0:T(8,128)S(1)} %get-tuple-element.29), channel_id=1, source_target_pairs={{0,5},{1,4},{2,7},{3,6},{4,1},{5,0},{6,3},{7,2},{8,13},{9,12},{10,... | collective-permute-start | bytes 24584 | tf_op jit(solution)/shard_map/ppermute | solution.py:396
  14.8 3.7 %collective-permute-start.7 = (f32[2,8,128]{2,1,0:T(8,128)S(1)}, f32[2,8,128]{2,1,0:T(8,128)S(1)}, u32[]{:S(2)}, u32[]{:S(2)}) collective-permute-start(f32[2,8,128]{2,1,0:T(8,128)S(1)} %get-tuple-element.30), channel_id=1, source_target_pairs={{0,1},{1,0},{2,3},{3,2},{4,5},{5,4},{6,7},{7,6},{8,9},{9,8},{10,11... | collective-permute-start | bytes 24584 | tf_op jit(solution)/shard_map/ppermute | solution.py:395

commit v6 on v5

--- a/solution.py
+++ b/solution.py
@@ -10,7 +10,7 @@
 LANES = 128
 ROWS = 8
 BLOCK = 3 * ROWS
-FAR = (1, 2, 3, 0)
+FAR = (((2, 3, 1, 0), (1, 2, 3, 0)), ((3, 2, 0, 1), (2, 3, 0, 1)), ((1, 0, 3, 2), (3, 0, 1, 2)), ((0, 1, 2, 3), (0, 1, 2, 3)))
 WHOLE = pl.BlockSpec(memory_space=pltpu.VMEM)
 PARAMS = pltpu.CompilerParams(vmem_limit_bytes=4 << 20)
 
@@ -48,12 +48,17 @@
         )
 
 
-def goal(rank, step, count):
-    return (rank + step) % count if step >= 0 else rank ^ -step
-
-
-def origin(rank, step, count):
-    return (rank + count - step) % count if step >= 0 else rank ^ -step
+def entry(tables, rank, core):
+    value = tables[0][0]
+    for c, table in enumerate(tables):
+        for place, item in enumerate(table):
+            if (c, place) != (0, 0):
+                value = jnp.where((rank == place) & (core == c), item, value)
+    return value
+
+
+def origins(tables):
+    return tuple(tuple(table.index(place) for place in range(len(table))) for table in tables)
 
 
 def load_kernel(dens_hbm, index_hbm, dens_ref, index_ref, dens_sem, index_sem):
@@ -104,7 +109,7 @@
     for group, side in enumerate(sides):
         scratch[group, ROWS] = side
     for step, out_ref in zip(FAR, outs):
-        out_ref[...] = scratch[goal(mine // 4, step, len(FAR))]
+        out_ref[...] = scratch[entry(step, mine // 4, core)]
 
 
 def second_kernel(*refs):
@@ -114,7 +119,7 @@
     place = mine // 2 % 2
     lane = lax.broadcasted_iota(jnp.int32, (ROWS, LANES), 1)
     for step, piece in zip(FAR, pieces):
-        group = origin(mine // 4, step, len(FAR))
+        group = entry(origins(step), mine // 4, mine % 2)
         packed = piece[ROWS]
         for x in range(2):
             for core in range(2):
@@ -381,8 +386,8 @@
     )
     came = []
     for value, step in zip(sent, FAR):
-        pairs = [(i, goal(i // 4, step, groups) * 4 + i % 4) for i in range(bricks)]
-        came.append(lax.ppermute(value, "depth", pairs) if step else value)
+        pairs = [(i, step[i % 2][i // 4] * 4 + i % 4) for i in range(bricks)]
+        came.append(lax.ppermute(value, "depth", pairs) if step != FAR[-1] else value)
     edge = jax.ShapeDtypeStruct((2, half, LANES), jnp.float32)
     keep, send, near, across = call(
         second_kernel,

time: 19.4 us -> 19.1 us (0.985)
  starting transfers between devices: 10.8 us -> 9.42 us
  waiting for transfers between devices: 5.1 us -> 6.16 us
    ppermute x3, starting transfers between devices: 6.7 us -> 5.36 us  [staged_body(): lax.ppermute(value, 'depth', pairs)]
    ppermute x3, waiting for transfers between devices: 2.61 us -> 3.67 us  [staged_body(): lax.ppermute(value, 'depth', pairs)]
where the time goes in v6:
time: 19.1 us; the launch traced here: 19 us
  starting transfers between devices  9.42 us (49%)
  waiting for transfers between devices  6.16 us (32%)
  Pallas kernels  3.35 us (18%)
    ppermute x3, starting transfers between devices, staged_body(): lax.ppermute(value, 'depth', pairs)  5.36 us
    ppermute x3, waiting for transfers between devices, staged_body(): lax.ppermute(value, 'depth', pairs)  3.67 us
    pallas_call x5, Pallas kernels, call(): pl.pallas_call(kernel, out_shape=out_shape, in_specs=[spec] * len(operand...  3.35 us
    ppermute x3, starting transfers between devices, swap(): return lax.ppermute(value, 'depth', [(i, i ^ mask) for i in range(bricks)])  2.07 us
    ppermute x1, starting transfers between devices, staged_body(): lax.ppermute(across, ('depth', 'gx'), [(2 * i + g, 2 * (i ^ 2) + 1 - g) f...  1.49 us
    ppermute x3, waiting for transfers between devices, swap(): return lax.ppermute(value, 'depth', [(i, i ^ mask) for i in range(bricks)])  1.46 us
    ppermute x1, waiting for transfers between devices, staged_body(): near = lax.ppermute(near, 'gx', [(0, 1), (1, 0)])  0.59 us
    ppermute x1, starting transfers between devices, staged_body(): near = lax.ppermute(near, 'gx', [(0, 1), (1, 0)])  0.51 us
  transfers between devices with their start and end apart: 8, of which 8 were waited for; matrix products, arithmetic and copies ran while one was open for 0% of the time, Pallas kernels for 11%

profile of v6, /device:TPU:0, one launch (start us, length us, event | category | flops | bytes accessed | tf_op | source)
XLA Modules:
  0.0 19.0 jit_solution(16491936586214752591)
XLA Ops:
  0.0 0.5 %collective-permute-start = (f32[2,8,1024]{2,1,0:T(8,128)}, f32[2,8,1024]{2,1,0:T(8,128)S(1)}, u32[]{:S(2)}, u32[]{:S(2)}) collective-permute-start(f32[2,8,1024]{2,1,0:T(8,128)} %dens_hbm.1), channel_id=1, source_target_pairs={{0,2},{2,0},{4,6},{6,4},{8,10},{10,8},{12,14},{14,12},{16,18},{18,... | collective-permute-start | bytes 196616 | tf_op jit(solution)/shard_map/ppermute | solution.py:367
  0.5 0.0 collective-permute-start.1
  0.5 0.9 %load.1 = (f32[2,8,1024]{2,1,0:T(8,128)S(1)}, s32[2,8,1024]{2,1,0:T(8,128)S(1)}) custom-call(f32[2,8,1024]{2,1,0:T(8,128)} %dens_hbm.1, s32[2,8,1024]{2,1,0:T(8,128)} %index_hbm.1), custom_call_target="tpu_custom_call" | custom-call | flops 1048576 | bytes 2097152 | tf_op jit(solution)/shard_map/load/pallas_call | solution.py:352
  1.4 0.2 %collective-permute-done.refs_2_ = f32[2,8,1024]{2,1,0:T(8,128)S(1)} collective-permute-done((f32[2,8,1024]{2,1,0:T(8,128)}, f32[2,8,1024]{2,1,0:T(8,128)S(1)}, u32[]{:S(2)}, u32[]{:S(2)}) %collective-permute-start) | collective-permute-done | bytes 65568 | tf_op jit(solution)/shard_map/ppermute | solution.py:367
  1.6 0.4 %collective-permute-done.1.refs_3_ = s32[2,8,1024]{2,1,0:T(8,128)S(1)} collective-permute-done((s32[2,8,1024]{2,1,0:T(8,128)}, s32[2,8,1024]{2,1,0:T(8,128)S(1)}, u32[]{:S(2)}, u32[]{:S(2)}) %collective-permute-start.1) | collective-permute-done | bytes 65568 | tf_op jit(solution)/shard_map/ppermute | solution.py:367
  2.0 0.2 %first.1 = (f32[9,8,128]{2,1,0:T(8,128)S(1)}, f32[9,8,128]{2,1,0:T(8,128)S(1)}, f32[9,8,128]{2,1,0:T(8,128)S(1)}, f32[9,8,128]{2,1,0:T(8,128)S(1)}) custom-call(f32[2,8,1024]{2,1,0:T(8,128)S(1)} %get-tuple-element.18.refs_0_, s32[2,8,1024]{2,1,0:T(8,128)S(1)} %get-tuple-element.19.refs_1_, f32[2,8,1024]{2,1,0:T(8,128)S(1)} %collective-permute-done.refs_2_, ...), custom_call_target="tpu_custom_call" | custom-call | tf_op jit(solution)/shard_map/first/pallas_call | solution.py:352
  2.2 3.8 %collective-permute-start.2 = (f32[9,8,128]{2,1,0:T(8,128)S(1)}, f32[9,8,128]{2,1,0:T(8,128)S(1)}, u32[]{:S(2)}, u32[]{:S(2)}) collective-permute-start(f32[9,8,128]{2,1,0:T(8,128)S(1)} %get-tuple-element.20), channel_id=1, source_target_pairs={{0,16},{2,10},{4,20},{6,14},{8,24},{10,18},{12,28},{14,22},{16,8},... | collective-permute-start | bytes 110600 | tf_op jit(solution)/shard_map/ppermute | solution.py:390
  6.0 1.1 %collective-permute-start.3 = (f32[9,8,128]{2,1,0:T(8,128)S(1)}, f32[9,8,128]{2,1,0:T(8,128)S(1)}, u32[]{:S(2)}, u32[]{:S(2)}) collective-permute-start(f32[9,8,128]{2,1,0:T(8,128)S(1)} %get-tuple-element.21), channel_id=1, source_target_pairs={{0,24},{2,18},{4,28},{6,22},{8,16},{10,26},{12,20},{14,30},{16,0},... | collective-permute-start | bytes 110600 | tf_op jit(solution)/shard_map/ppermute | solution.py:390
  7.0 0.5 %collective-permute-start.4 = (f32[9,8,128]{2,1,0:T(8,128)S(1)}, f32[9,8,128]{2,1,0:T(8,128)S(1)}, u32[]{:S(2)}, u32[]{:S(2)}) collective-permute-start(f32[9,8,128]{2,1,0:T(8,128)S(1)} %get-tuple-element.22), channel_id=1, source_target_pairs={{0,8},{2,26},{4,12},{6,30},{8,0},{10,2},{12,4},{14,6},{16,24},{18,... | collective-permute-start | bytes 110600 | tf_op jit(solution)/shard_map/ppermute | solution.py:390
  7.5 1.5 %collective-permute-done.2.refs_0_ = f32[9,8,128]{2,1,0:T(8,128)S(1)} collective-permute-done((f32[9,8,128]{2,1,0:T(8,128)S(1)}, f32[9,8,128]{2,1,0:T(8,128)S(1)}, u32[]{:S(2)}, u32[]{:S(2)}) %collective-permute-start.2) | collective-permute-done | bytes 36896 | tf_op jit(solution)/shard_map/ppermute | solution.py:390
  9.1 1.8 %collective-permute-done.3.refs_1_ = f32[9,8,128]{2,1,0:T(8,128)S(1)} collective-permute-done((f32[9,8,128]{2,1,0:T(8,128)S(1)}, f32[9,8,128]{2,1,0:T(8,128)S(1)}, u32[]{:S(2)}, u32[]{:S(2)}) %collective-permute-start.3) | collective-permute-done | bytes 36896 | tf_op jit(solution)/shard_map/ppermute | solution.py:390
  10.8 0.4 %collective-permute-done.4.refs_2_ = f32[9,8,128]{2,1,0:T(8,128)S(1)} collective-permute-done((f32[9,8,128]{2,1,0:T(8,128)S(1)}, f32[9,8,128]{2,1,0:T(8,128)S(1)}, u32[]{:S(2)}, u32[]{:S(2)}) %collective-permute-start.4) | collective-permute-done | bytes 36896 | tf_op jit(solution)/shard_map/ppermute | solution.py:390
  11.2 0.2 second.1
  11.4 0.0 copy-start
  11.4 1.6 %collective-permute-start.5 = (f32[17,8,128]{2,1,0:T(8,128)S(1)}, f32[17,8,128]{2,1,0:T(8,128)S(1)}, u32[]{:S(2)}, u32[]{:S(2)}) collective-permute-start(f32[17,8,128]{2,1,0:T(8,128)S(1)} %get-tuple-element.25), channel_id=1, source_target_pairs={{0,4},{2,6},{4,0},{6,2},{8,12},{10,14},{12,8},{14,10},{16,20},{18,... | collective-permute-start | bytes 208904 | tf_op jit(solution)/shard_map/ppermute | solution.py:367
  13.0 1.5 %collective-permute-start.6 = (f32[2,8,128]{2,1,0:T(8,128)S(1)}, f32[2,8,128]{2,1,0:T(8,128)S(1)}, u32[]{:S(2)}, u32[]{:S(2)}) collective-permute-start(f32[2,8,128]{2,1,0:T(8,128)S(1)} %get-tuple-element.29), channel_id=1, source_target_pairs={{0,5},{1,4},{2,7},{3,6},{4,1},{5,0},{6,3},{7,2},{8,13},{9,12},{10,... | collective-permute-start | bytes 24584 | tf_op jit(solution)/shard_map/ppermute | solution.py:401
  14.5 0.5 %collective-permute-start.7 = (f32[2,8,128]{2,1,0:T(8,128)S(1)}, f32[2,8,128]{2,1,0:T(8,128)S(1)}, u32[]{:S(2)}, u32[]{:S(2)}) collective-permute-start(f32[2,8,128]{2,1,0:T(8,128)S(1)} %get-tuple-element.30), channel_id=1, source_target_pairs={{0,1},{1,0},{2,3},{3,2},{4,5},{5,4},{6,7},{7,6},{8,9},{9,8},{10,11... | collective-permute-start | bytes 24584 | tf_op jit(solution)/shard_map/ppermute | solution.py:400
  15.0 0.9 %collective-permute-done.5.came_ref = f32[17,8,128]{2,1,0:T(8,128)S(1)} collective-permute-done((f32[17,8,128]{2,1,0:T(8,128)S(1)}, f32[17,8,128]{2,1,0:T(8,128)S(1)}, u32[]{:S(2)}, u32[]{:S(2)}) %collective-permute-start.5) | collective-permute-done | bytes 69664 | tf_op jit(solution)/shard_map/ppermute | solution.py:367
  15.9 0.0 copy-done
  15.9 1.2 %render.1 = (f32[4,8,128]{2,1,0:T(8,128)S(1)}, f32[3,16,8,128]{3,2,1,0:T(8,128)S(1)}, f32[3,16,8,128]{3,2,1,0:T(8,128)S(1)}) custom-call(f32[8,24,128]{2,1,0:T(8,128)S(1)} %get-tuple-element.24.keep_ref, f32[17,8,128]{2,1,0:T(8,128)S(1)} %collective-permute-done.5.came_ref, f32[4,256]{1,0:T(4,128)S(1)} %copy-done), custom_call_target="tpu_custom_call" | custom-call | flops 16777216 | bytes 8388608 | tf_op jit(solution)/shard_map/render/pallas_call | solution.py:352
  17.1 0.4 %collective-permute-done.6.across_ref = f32[2,8,128]{2,1,0:T(8,128)S(1)} collective-permute-done((f32[2,8,128]{2,1,0:T(8,128)S(1)}, f32[2,8,128]{2,1,0:T(8,128)S(1)}, u32[]{:S(2)}, u32[]{:S(2)}) %collective-permute-start.6) | collective-permute-done | bytes 8224 | tf_op jit(solution)/shard_map/ppermute | solution.py:401
  17.5 0.6 %collective-permute-done.7.near_ref = f32[2,8,128]{2,1,0:T(8,128)S(1)} collective-permute-done((f32[2,8,128]{2,1,0:T(8,128)S(1)}, f32[2,8,128]{2,1,0:T(8,128)S(1)}, u32[]{:S(2)}, u32[]{:S(2)}) %collective-permute-start.7) | collective-permute-done | bytes 8224 | tf_op jit(solution)/shard_map/ppermute | solution.py:400
  18.1 0.9 %finish.1 = f32[4,8,64]{2,1,0:T(8,128)} custom-call(f32[4,8,128]{2,1,0:T(8,128)S(1)} %get-tuple-element.26.image_ref, f32[3,16,8,128]{3,2,1,0:T(8,128)S(1)} %get-tuple-element.27.grad_ref, f32[3,16,8,128]{3,2,1,0:T(8,128)S(1)} %get-tuple-element.28.weight_ref, f32[2,8,128]{2,1,0:T(8,128)S(1)} %collective-permute-done.6.across_ref, ...), custom_call_target="tpu_custom_call" | custom-call | tf_op jit(solution)/shard_map/finish/pallas_call | solution.py:352
Async XLA Ops:
  0.0 1.6 %collective-permute-start = (f32[2,8,1024]{2,1,0:T(8,128)}, f32[2,8,1024]{2,1,0:T(8,128)S(1)}, u32[]{:S(2)}, u32[]{:S(2)}) collective-permute-start(f32[2,8,1024]{2,1,0:T(8,128)} %dens_hbm.1), channel_id=1, source_target_pairs={{0,2},{2,0},{4,6},{6,4},{8,10},{10,8},{12,14},{14,12},{16,18},{18,... | collective-permute-start | bytes 196616 | tf_op jit(solution)/shard_map/ppermute | solution.py:367
  0.5 1.5 %collective-permute-start.1 = (s32[2,8,1024]{2,1,0:T(8,128)}, s32[2,8,1024]{2,1,0:T(8,128)S(1)}, u32[]{:S(2)}, u32[]{:S(2)}) collective-permute-start(s32[2,8,1024]{2,1,0:T(8,128)} %index_hbm.1), channel_id=1, source_target_pairs={{0,2},{2,0},{4,6},{6,4},{8,10},{10,8},{12,14},{14,12},{16,18},{18,... | collective-permute-start | bytes 196616 | tf_op jit(solution)/shard_map/ppermute | solution.py:367
  2.2 6.9 %collective-permute-start.2 = (f32[9,8,128]{2,1,0:T(8,128)S(1)}, f32[9,8,128]{2,1,0:T(8,128)S(1)}, u32[]{:S(2)}, u32[]{:S(2)}) collective-permute-start(f32[9,8,128]{2,1,0:T(8,128)S(1)} %get-tuple-element.20), channel_id=1, source_target_pairs={{0,16},{2,10},{4,20},{6,14},{8,24},{10,18},{12,28},{14,22},{16,8},... | collective-permute-start | bytes 110600 | tf_op jit(solution)/shard_map/ppermute | solution.py:390
  6.0 4.9 %collective-permute-start.3 = (f32[9,8,128]{2,1,0:T(8,128)S(1)}, f32[9,8,128]{2,1,0:T(8,128)S(1)}, u32[]{:S(2)}, u32[]{:S(2)}) collective-permute-start(f32[9,8,128]{2,1,0:T(8,128)S(1)} %get-tuple-element.21), channel_id=1, source_target_pairs={{0,24},{2,18},{4,28},{6,22},{8,16},{10,26},{12,20},{14,30},{16,0},... | collective-permute-start | bytes 110600 | tf_op jit(solution)/shard_map/ppermute | solution.py:390
  7.0 4.2 %collective-permute-start.4 = (f32[9,8,128]{2,1,0:T(8,128)S(1)}, f32[9,8,128]{2,1,0:T(8,128)S(1)}, u32[]{:S(2)}, u32[]{:S(2)}) collective-permute-start(f32[9,8,128]{2,1,0:T(8,128)S(1)} %get-tuple-element.22), channel_id=1, source_target_pairs={{0,8},{2,26},{4,12},{6,30},{8,0},{10,2},{12,4},{14,6},{16,24},{18,... | collective-permute-start | bytes 110600 | tf_op jit(solution)/shard_map/ppermute | solution.py:390
  11.4 4.5 %copy-start = (f32[4,256]{1,0:T(4,128)S(1)}, f32[4,256]{1,0:T(4,128)}, u32[]{:S(2)}) copy-start(f32[4,256]{1,0:T(4,128)} %table_ref.1) | copy-start | bytes 12292
  11.4 4.5 %collective-permute-start.5 = (f32[17,8,128]{2,1,0:T(8,128)S(1)}, f32[17,8,128]{2,1,0:T(8,128)S(1)}, u32[]{:S(2)}, u32[]{:S(2)}) collective-permute-start(f32[17,8,128]{2,1,0:T(8,128)S(1)} %get-tuple-element.25), channel_id=1, source_target_pairs={{0,4},{2,6},{4,0},{6,2},{8,12},{10,14},{12,8},{14,10},{16,20},{18,... | collective-permute-start | bytes 208904 | tf_op jit(solution)/shard_map/ppermute | solution.py:367
  13.0 4.5 %collective-permute-start.6 = (f32[2,8,128]{2,1,0:T(8,128)S(1)}, f32[2,8,128]{2,1,0:T(8,128)S(1)}, u32[]{:S(2)}, u32[]{:S(2)}) collective-permute-start(f32[2,8,128]{2,1,0:T(8,128)S(1)} %get-tuple-element.29), channel_id=1, source_target_pairs={{0,5},{1,4},{2,7},{3,6},{4,1},{5,0},{6,3},{7,2},{8,13},{9,12},{10,... | collective-permute-start | bytes 24584 | tf_op jit(solution)/shard_map/ppermute | solution.py:401
  14.5 3.7 %collective-permute-start.7 = (f32[2,8,128]{2,1,0:T(8,128)S(1)}, f32[2,8,128]{2,1,0:T(8,128)S(1)}, u32[]{:S(2)}, u32[]{:S(2)}) collective-permute-start(f32[2,8,128]{2,1,0:T(8,128)S(1)} %get-tuple-element.30), channel_id=1, source_target_pairs={{0,1},{1,0},{2,3},{3,2},{4,5},{5,4},{6,7},{7,6},{8,9},{9,8},{10,11... | collective-permute-start | bytes 24584 | tf_op jit(solution)/shard_map/ppermute | solution.py:400

commit v7 on v6

--- a/solution.py
+++ b/solution.py
@@ -6,6 +6,7 @@
 from jax.experimental import pallas as pl
 from jax.experimental.pallas import tpu as pltpu
 from jax.sharding import PartitionSpec as P
+
 
 LANES = 128
 ROWS = 8
@@ -71,7 +72,7 @@
 
 
 def first_kernel(*refs):
-    own, other, outs, scratch = refs[0:2], refs[2:4], refs[4:-1], refs[-1]
+    own, other, outs, scratch = refs[0:2], refs[2], refs[3:-1], refs[-1]
     half = LANES // 2
     mine = lax.axis_index("depth")
     core = mine % 2
@@ -83,17 +84,22 @@
     def tile_of(ref, layer, m):
         return ref[layer, :, m * LANES : (m + 1) * LANES] if 0 <= m < tiles else zero
 
-    def pair(values):
+    def pair(values, core):
         first = pltpu.roll(values[0], half * core, 1)
         return jnp.where(lane < half, first, pltpu.roll(values[1], half * (1 - core), 1))
 
-    for n, (dens_ref, index_ref) in enumerate((own, other)):
+    for m in range(tiles):
+        group, place = divmod(m, 2)
+        index = [tile_of(own[1], layer, m).astype(jnp.float32) for layer in range(2)]
+        scratch[group, 4 * place + 2] = jnp.where(lane < half, index[0], pltpu.roll(index[1], half, 1))
+        scratch[group, 4 * place + 3] = jnp.where(lane < half, pltpu.roll(index[0], half, 1), index[1])
+
+    for n, dens_ref in enumerate((own[0], other)):
         slot = core ^ n
         for m in range(tiles):
             group, place = divmod(m, 2)
-            scratch[group, 4 * place + slot] = pair([tile_of(dens_ref, layer, m) for layer in range(2)])
-            scratch[group, 4 * place + 2 + slot] = pair(
-                [tile_of(index_ref, layer, m).astype(jnp.float32) for layer in range(2)]
+            scratch[group, 4 * place + slot] = pair(
+                [tile_of(dens_ref, layer, m) for layer in range(2)], core
             )
             brick = 2 * place + slot
             for layer in range(2):
@@ -113,7 +119,8 @@
 
 
 def second_kernel(*refs):
-    pieces, (keep_ref, send_ref, near_ref, across_ref, scratch) = refs[: len(FAR)], refs[len(FAR) :]
+    pieces, refs = refs[: len(FAR)], refs[len(FAR) :]
+    keep_ref, index_ref, send_ref, near_ref, across_ref, scratch, index_scratch = refs
     half = LANES // 2
     mine = lax.axis_index("depth")
     place = mine // 2 % 2
@@ -128,14 +135,15 @@
                 first = pltpu.roll(packed, LANES - p, 1) if p else packed
                 last = pltpu.roll(packed, p, 1) if p else packed
                 scratch[x, brick, 0:ROWS] = piece[4 * x + core]
-                scratch[x, brick, ROWS : 2 * ROWS] = piece[4 * x + 2 + core]
+                index_scratch[x, core, group] = piece[4 * x + 2 + core]
                 scratch[x, brick, 2 * ROWS :] = jnp.where(lane % half == 0, first, last)
     bricks = scratch.shape[1]
     sides = jnp.zeros((ROWS, LANES), jnp.float32)
     for brick in range(bricks):
         keep_ref[brick] = scratch[place, brick]
         send_ref[brick] = scratch[1 - place, brick, 0:ROWS]
-        send_ref[bricks + brick] = scratch[1 - place, brick, ROWS : 2 * ROWS]
+        index_ref[brick // 4, brick % 4] = index_scratch[place, brick // 4, brick % 4]
+        send_ref[bricks + brick] = index_scratch[1 - place, brick // 4, brick % 4]
         side = scratch[1 - place, brick, 2 * ROWS :]
         first = pltpu.roll(side, brick, 1) if brick else side
         last = pltpu.roll(side, LANES - brick, 1) if brick else side
@@ -149,7 +157,15 @@
             ref[part] = jnp.where(top, scratch[x, :, low + ROWS - 1, :], scratch[x, :, low, :])
 
 
-def staged_render_kernel(width, step_len, keep_ref, came_ref, table_ref, *refs):
+def index_kernel(index_ref, came_ref, out_ref):
+    other = 1 - lax.axis_index("depth") % 2
+    groups = index_ref.shape[1]
+    for group in range(groups):
+        out_ref[group] = index_ref[other, group]
+        out_ref[groups + group] = came_ref[4 * groups // 2 + groups * other + group]
+
+
+def staged_render_kernel(width, step_len, keep_ref, came_ref, index_ref, given_ref, table_ref, *refs):
     outs, got_ref = refs[:-1], refs[-1]
     half = LANES // 2
     place = lax.axis_index("depth") // 2 % 2
@@ -163,8 +179,15 @@
         first = pltpu.roll(packed, LANES - brick, 1) if brick else packed
         last = pltpu.roll(packed, brick, 1) if brick else packed
         got_ref[target, 0:ROWS] = came_ref[brick]
-        got_ref[target, ROWS : 2 * ROWS] = came_ref[bricks + brick]
         got_ref[target, 2 * ROWS :] = jnp.where(lane % half == 0, first, last)
+    mine = lax.axis_index("depth") % 2
+    for group in range(bricks // 2):
+        for core, near, far in (
+            (mine, index_ref[mine, group], came_ref[bricks + bricks // 2 * mine + group]),
+            (1 - mine, given_ref[group], given_ref[bricks // 2 + group]),
+        ):
+            got_ref[4 * group + 2 * place + core, ROWS : 2 * ROWS] = near
+            got_ref[4 * group + 2 * (1 - place) + core, ROWS : 2 * ROWS] = far
     render_kernel(width, step_len, got_ref, table_ref, *outs)
 
 
@@ -348,7 +371,7 @@
     step_len = 1.0 / (layers * bricks)
     half = bricks // 2
 
-    def call(kernel, out_shape, operands, name, scratch=(), cost=None, spec=WHOLE):
+    def call(kernel, out_shape, operands, scratch=(), cost=None, spec=WHOLE):
         return pl.pallas_call(
             kernel,
             out_shape=out_shape,
@@ -356,7 +379,6 @@
             out_specs=jax.tree.map(lambda _: WHOLE, out_shape),
             scratch_shapes=scratch,
             cost_estimate=cost,
-            name=name,
             compiler_params=PARAMS,
         )(*operands)
 
@@ -367,12 +389,11 @@
         return lax.ppermute(value, "depth", [(i, i ^ mask) for i in range(bricks)])
 
     inputs = [pltpu.with_memory_space_constraint(a, pltpu.HBM) for a in (density, tf_index)]
-    theirs = [swap(value, 1) for value in (density, tf_index)]
+    theirs = swap(density, 1)
     ours = call(
         load_kernel,
         [jax.ShapeDtypeStruct(a.shape, a.dtype) for a in inputs],
         inputs,
-        "load",
         [pltpu.SemaphoreType.DMA] * 2,
         pl.CostEstimate(flops=1 << 20, bytes_accessed=1 << 21, transcendentals=0),
         pl.BlockSpec(memory_space=pltpu.HBM),
@@ -380,8 +401,7 @@
     sent = call(
         first_kernel,
         [block(ROWS + 1)] * groups,
-        [*ours, *theirs],
-        "first",
+        [*ours, theirs],
         [pltpu.VMEM((groups, ROWS + 1, ROWS, LANES), jnp.float32)],
     )
     came = []
@@ -389,24 +409,27 @@
         pairs = [(i, step[i % 2][i // 4] * 4 + i % 4) for i in range(bricks)]
         came.append(lax.ppermute(value, "depth", pairs) if step != FAR[-1] else value)
     edge = jax.ShapeDtypeStruct((2, half, LANES), jnp.float32)
-    keep, send, near, across = call(
+    keep, index, send, near, across = call(
         second_kernel,
-        [jax.ShapeDtypeStruct((half, BLOCK, LANES), jnp.float32), block(2 * half + 1), edge, edge],
+        [jax.ShapeDtypeStruct((half, BLOCK, LANES), jnp.float32), block(2, groups), block(2 * half + 1), edge, edge],
         came,
-        "second",
-        [pltpu.VMEM((2, half, BLOCK, LANES), jnp.float32)],
+        [
+            pltpu.VMEM((2, half, BLOCK, LANES), jnp.float32),
+            pltpu.VMEM((2, 2, groups, ROWS, LANES), jnp.float32),
+        ],
     )
     other = swap(send, 2)
     near = lax.ppermute(near, "gx", [(0, 1), (1, 0)])
     across = lax.ppermute(
         across, ("depth", "gx"), [(2 * i + g, 2 * (i ^ 2) + 1 - g) for i in range(bricks) for g in range(2)]
     )
+    given = call(index_kernel, block(half), [index, other])
+    given = swap(given, 1)
     voxels = block(3, bricks)
     parts = call(
         functools.partial(staged_render_kernel, width, step_len),
         [block(4), voxels, voxels],
-        [keep, other, tf_table],
-        "render",
+        [keep, other, index, given, tf_table],
         [pltpu.VMEM((bricks, BLOCK, LANES), jnp.float32)],
         pl.CostEstimate(flops=1 << 24, bytes_accessed=1 << 23, transcendentals=0),
     )
@@ -414,7 +437,6 @@
         functools.partial(staged_finish_kernel, width),
         jax.ShapeDtypeStruct((4, rows, width), jnp.float32),
         [*parts, across, near],
-        "finish",
         [pltpu.VMEM((2, bricks, LANES), jnp.float32)],
     )
 

time: 19.1 us -> 22.8 us (1.19)
  waiting for transfers between devices: 6.16 us -> 8.89 us
  starting transfers between devices: 9.42 us -> 10.6 us
  Pallas kernels: 3.35 us -> 3.09 us
    ppermute x3, waiting for transfers between devices: 1.46 us -> 3.04 us  [swap(): return lax.ppermute(value, 'depth', [(i, i ^ mask) for i in range(bricks)])]
    ppermute x1, starting transfers between devices: 1.49 us -> 2.52 us  [staged_body(): lax.ppermute(across, ('depth', 'gx'), [(2 * i + g, 2 * (i ^ 2) + 1 - g) f...]
    ppermute x1, waiting for transfers between devices: 0.59 us -> 1.55 us  [staged_body(): near = lax.ppermute(near, 'gx', [(0, 1), (1, 0)])]
    pallas_call x5 -> x6, Pallas kernels: 3.35 us -> 3.09 us  [call(): pl.pallas_call(kernel, out_shape=out_shape, in_specs=[spec] * len(operand...]
  transfers between devices with their start and end apart: 8 -> 8, of which waited for: 8 -> 7; matrix products, arithmetic and copies ran while one was open for 0% -> 0% of each run, Pallas kernels for 11% -> 8%
where the time goes in v7:
time: 22.8 us; the launch traced here: 22.7 us
  starting transfers between devices  10.6 us (46%)
  waiting for transfers between devices  8.89 us (39%)
  Pallas kernels  3.09 us (14%)
    ppermute x3, starting transfers between devices, staged_body(): lax.ppermute(value, 'depth', pairs)  5.56 us
    ppermute x3, waiting for transfers between devices, staged_body(): lax.ppermute(value, 'depth', pairs)  3.67 us
    pallas_call x6, Pallas kernels, call(): pl.pallas_call(kernel, out_shape=out_shape, in_specs=[spec] * len(operand...  3.09 us
    ppermute x3, waiting for transfers between devices, swap(): return lax.ppermute(value, 'depth', [(i, i ^ mask) for i in range(bricks)])  3.04 us
    ppermute x1, starting transfers between devices, staged_body(): lax.ppermute(across, ('depth', 'gx'), [(2 * i + g, 2 * (i ^ 2) + 1 - g) f...  2.52 us
    ppermute x3, starting transfers between devices, swap(): return lax.ppermute(value, 'depth', [(i, i ^ mask) for i in range(bricks)])  2.05 us
    ppermute x1, waiting for transfers between devices, staged_body(): near = lax.ppermute(near, 'gx', [(0, 1), (1, 0)])  1.55 us
    ppermute x1, waiting for transfers between devices, staged_body(): lax.ppermute(across, ('depth', 'gx'), [(2 * i + g, 2 * (i ^ 2) + 1 - g) f...  0.64 us
  transfers between devices with their start and end apart: 8, of which 7 were waited for; matrix products, arithmetic and copies ran while one was open for 0% of the time, Pallas kernels for 8%

profile of v7, /device:TPU:0, one launch (start us, length us, event | category | flops | bytes accessed | tf_op | source)
XLA Modules:
  0.0 22.7 jit_solution(4690980538312183350)
XLA Ops:
  0.0 0.5 %collective-permute-start = (f32[2,8,1024]{2,1,0:T(8,128)}, f32[2,8,1024]{2,1,0:T(8,128)S(1)}, u32[]{:S(2)}, u32[]{:S(2)}) collective-permute-start(f32[2,8,1024]{2,1,0:T(8,128)} %dens_hbm.1), channel_id=1, source_target_pairs={{0,2},{2,0},{4,6},{6,4},{8,10},{10,8},{12,14},{14,12},{16,18},{18,... | collective-permute-start | bytes 196616 | tf_op jit(solution)/shard_map/ppermute | solution.py:389
  0.5 0.9 %shard_map.37 = (f32[2,8,1024]{2,1,0:T(8,128)S(1)}, s32[2,8,1024]{2,1,0:T(8,128)S(1)}) custom-call(f32[2,8,1024]{2,1,0:T(8,128)} %dens_hbm.1, s32[2,8,1024]{2,1,0:T(8,128)} %index_hbm.1), custom_call_target="tpu_custom_call" | custom-call | flops 1048576 | bytes 2097152 | tf_op jit(solution)/shard_map/pallas_call | solution.py:375
  1.4 0.2 collective-permute-done.refs_2_
  1.6 0.2 shard_map.38
  1.8 4.0 %collective-permute-start.1 = (f32[9,8,128]{2,1,0:T(8,128)S(1)}, f32[9,8,128]{2,1,0:T(8,128)S(1)}, u32[]{:S(2)}, u32[]{:S(2)}) collective-permute-start(f32[9,8,128]{2,1,0:T(8,128)S(1)} %get-tuple-element.21), channel_id=1, source_target_pairs={{0,16},{2,10},{4,20},{6,14},{8,24},{10,18},{12,28},{14,22},{16,8},... | collective-permute-start | bytes 110600 | tf_op jit(solution)/shard_map/ppermute | solution.py:410
  5.8 1.1 %collective-permute-start.2 = (f32[9,8,128]{2,1,0:T(8,128)S(1)}, f32[9,8,128]{2,1,0:T(8,128)S(1)}, u32[]{:S(2)}, u32[]{:S(2)}) collective-permute-start(f32[9,8,128]{2,1,0:T(8,128)S(1)} %get-tuple-element.22), channel_id=1, source_target_pairs={{0,24},{2,18},{4,28},{6,22},{8,16},{10,26},{12,20},{14,30},{16,0},... | collective-permute-start | bytes 110600 | tf_op jit(solution)/shard_map/ppermute | solution.py:410
  6.9 0.5 %collective-permute-start.3 = (f32[9,8,128]{2,1,0:T(8,128)S(1)}, f32[9,8,128]{2,1,0:T(8,128)S(1)}, u32[]{:S(2)}, u32[]{:S(2)}) collective-permute-start(f32[9,8,128]{2,1,0:T(8,128)S(1)} %get-tuple-element.23), channel_id=1, source_target_pairs={{0,8},{2,26},{4,12},{6,30},{8,0},{10,2},{12,4},{14,6},{16,24},{18,... | collective-permute-start | bytes 110600 | tf_op jit(solution)/shard_map/ppermute | solution.py:410
  7.4 1.4 %collective-permute-done.1.refs_0_ = f32[9,8,128]{2,1,0:T(8,128)S(1)} collective-permute-done((f32[9,8,128]{2,1,0:T(8,128)S(1)}, f32[9,8,128]{2,1,0:T(8,128)S(1)}, u32[]{:S(2)}, u32[]{:S(2)}) %collective-permute-start.1) | collective-permute-done | bytes 36896 | tf_op jit(solution)/shard_map/ppermute | solution.py:410
  8.8 1.9 %collective-permute-done.2.refs_1_ = f32[9,8,128]{2,1,0:T(8,128)S(1)} collective-permute-done((f32[9,8,128]{2,1,0:T(8,128)S(1)}, f32[9,8,128]{2,1,0:T(8,128)S(1)}, u32[]{:S(2)}, u32[]{:S(2)}) %collective-permute-start.2) | collective-permute-done | bytes 36896 | tf_op jit(solution)/shard_map/ppermute | solution.py:410
  10.7 0.4 %collective-permute-done.3.refs_2_ = f32[9,8,128]{2,1,0:T(8,128)S(1)} collective-permute-done((f32[9,8,128]{2,1,0:T(8,128)S(1)}, f32[9,8,128]{2,1,0:T(8,128)S(1)}, u32[]{:S(2)}, u32[]{:S(2)}) %collective-permute-start.3) | collective-permute-done | bytes 36896 | tf_op jit(solution)/shard_map/ppermute | solution.py:410
  11.1 0.2 shard_map.39
  11.2 1.6 %collective-permute-start.4 = (f32[17,8,128]{2,1,0:T(8,128)S(1)}, f32[17,8,128]{2,1,0:T(8,128)S(1)}, u32[]{:S(2)}, u32[]{:S(2)}) collective-permute-start(f32[17,8,128]{2,1,0:T(8,128)S(1)} %get-tuple-element.26), channel_id=1, source_target_pairs={{0,4},{2,6},{4,0},{6,2},{8,12},{10,14},{12,8},{14,10},{16,20},{18,... | collective-permute-start | bytes 208904 | tf_op jit(solution)/shard_map/ppermute | solution.py:389
  12.8 2.8 %collective-permute-done.4.came_ref = f32[17,8,128]{2,1,0:T(8,128)S(1)} collective-permute-done((f32[17,8,128]{2,1,0:T(8,128)S(1)}, f32[17,8,128]{2,1,0:T(8,128)S(1)}, u32[]{:S(2)}, u32[]{:S(2)}) %collective-permute-start.4) | collective-permute-done | bytes 69664 | tf_op jit(solution)/shard_map/ppermute | solution.py:389
  15.6 0.0 copy-start
  15.6 0.0 collective-permute-start.5
  15.6 2.5 %collective-permute-start.6 = (f32[2,8,128]{2,1,0:T(8,128)S(1)}, f32[2,8,128]{2,1,0:T(8,128)S(1)}, u32[]{:S(2)}, u32[]{:S(2)}) collective-permute-start(f32[2,8,128]{2,1,0:T(8,128)S(1)} %get-tuple-element.31), channel_id=1, source_target_pairs={{0,5},{1,4},{2,7},{3,6},{4,1},{5,0},{6,3},{7,2},{8,13},{9,12},{10,... | collective-permute-start | bytes 24584 | tf_op jit(solution)/shard_map/ppermute | solution.py:423
  18.1 0.5 %collective-permute-start.7 = (f32[2,8,128]{2,1,0:T(8,128)S(1)}, f32[2,8,128]{2,1,0:T(8,128)S(1)}, u32[]{:S(2)}, u32[]{:S(2)}) collective-permute-start(f32[2,8,128]{2,1,0:T(8,128)S(1)} %get-tuple-element.32), channel_id=1, source_target_pairs={{0,1},{1,0},{2,3},{3,2},{4,5},{5,4},{6,7},{7,6},{8,9},{9,8},{10,11... | collective-permute-start | bytes 24584 | tf_op jit(solution)/shard_map/ppermute | solution.py:422
  18.6 0.0 collective-permute-done.5.given_ref
  18.6 0.0 copy-done
  18.7 1.0 %shard_map.41 = (f32[4,8,128]{2,1,0:T(8,128)S(1)}, f32[3,16,8,128]{3,2,1,0:T(8,128)S(1)}, f32[3,16,8,128]{3,2,1,0:T(8,128)S(1)}) custom-call(f32[8,24,128]{2,1,0:T(8,128)S(1)} %get-tuple-element.25.keep_ref, f32[17,8,128]{2,1,0:T(8,128)S(1)} %collective-permute-done.4.came_ref, f32[2,4,8,128]{3,2,1,0:T(8,128)S(1)} %get-tuple-element.27.index_ref, ...), custom_call_target="tpu_custom_call" | custom-call | flops 16777216 | bytes 8388608 | tf_op jit(solution)/shard_map/pallas_call | solution.py:375
  19.6 0.6 %collective-permute-done.6.across_ref = f32[2,8,128]{2,1,0:T(8,128)S(1)} collective-permute-done((f32[2,8,128]{2,1,0:T(8,128)S(1)}, f32[2,8,128]{2,1,0:T(8,128)S(1)}, u32[]{:S(2)}, u32[]{:S(2)}) %collective-permute-start.6) | collective-permute-done | bytes 8224 | tf_op jit(solution)/shard_map/ppermute | solution.py:423
  20.2 1.6 %collective-permute-done.7.near_ref = f32[2,8,128]{2,1,0:T(8,128)S(1)} collective-permute-done((f32[2,8,128]{2,1,0:T(8,128)S(1)}, f32[2,8,128]{2,1,0:T(8,128)S(1)}, u32[]{:S(2)}, u32[]{:S(2)}) %collective-permute-start.7) | collective-permute-done | bytes 8224 | tf_op jit(solution)/shard_map/ppermute | solution.py:422
  21.8 0.9 %shard_map.42 = f32[4,8,64]{2,1,0:T(8,128)} custom-call(f32[4,8,128]{2,1,0:T(8,128)S(1)} %get-tuple-element.28.image_ref, f32[3,16,8,128]{3,2,1,0:T(8,128)S(1)} %get-tuple-element.29.grad_ref, f32[3,16,8,128]{3,2,1,0:T(8,128)S(1)} %get-tuple-element.30.weight_ref, f32[2,8,128]{2,1,0:T(8,128)S(1)} %collective-permute-done.6.across_ref, ...), custom_call_target="tpu_custom_call" | custom-call | tf_op jit(solution)/shard_map/pallas_call | solution.py:375
  (1 shorter events, 0.0 us)
Async XLA Ops:
  0.0 1.6 %collective-permute-start = (f32[2,8,1024]{2,1,0:T(8,128)}, f32[2,8,1024]{2,1,0:T(8,128)S(1)}, u32[]{:S(2)}, u32[]{:S(2)}) collective-permute-start(f32[2,8,1024]{2,1,0:T(8,128)} %dens_hbm.1), channel_id=1, source_target_pairs={{0,2},{2,0},{4,6},{6,4},{8,10},{10,8},{12,14},{14,12},{16,18},{18,... | collective-permute-start | bytes 196616 | tf_op jit(solution)/shard_map/ppermute | solution.py:389
  1.8 6.9 %collective-permute-start.1 = (f32[9,8,128]{2,1,0:T(8,128)S(1)}, f32[9,8,128]{2,1,0:T(8,128)S(1)}, u32[]{:S(2)}, u32[]{:S(2)}) collective-permute-start(f32[9,8,128]{2,1,0:T(8,128)S(1)} %get-tuple-element.21), channel_id=1, source_target_pairs={{0,16},{2,10},{4,20},{6,14},{8,24},{10,18},{12,28},{14,22},{16,8},... | collective-permute-start | bytes 110600 | tf_op jit(solution)/shard_map/ppermute | solution.py:410
  5.8 4.9 %collective-permute-start.2 = (f32[9,8,128]{2,1,0:T(8,128)S(1)}, f32[9,8,128]{2,1,0:T(8,128)S(1)}, u32[]{:S(2)}, u32[]{:S(2)}) collective-permute-start(f32[9,8,128]{2,1,0:T(8,128)S(1)} %get-tuple-element.22), channel_id=1, source_target_pairs={{0,24},{2,18},{4,28},{6,22},{8,16},{10,26},{12,20},{14,30},{16,0},... | collective-permute-start | bytes 110600 | tf_op jit(solution)/shard_map/ppermute | solution.py:410
  6.9 4.2 %collective-permute-start.3 = (f32[9,8,128]{2,1,0:T(8,128)S(1)}, f32[9,8,128]{2,1,0:T(8,128)S(1)}, u32[]{:S(2)}, u32[]{:S(2)}) collective-permute-start(f32[9,8,128]{2,1,0:T(8,128)S(1)} %get-tuple-element.23), channel_id=1, source_target_pairs={{0,8},{2,26},{4,12},{6,30},{8,0},{10,2},{12,4},{14,6},{16,24},{18,... | collective-permute-start | bytes 110600 | tf_op jit(solution)/shard_map/ppermute | solution.py:410
  11.2 4.4 %collective-permute-start.4 = (f32[17,8,128]{2,1,0:T(8,128)S(1)}, f32[17,8,128]{2,1,0:T(8,128)S(1)}, u32[]{:S(2)}, u32[]{:S(2)}) collective-permute-start(f32[17,8,128]{2,1,0:T(8,128)S(1)} %get-tuple-element.26), channel_id=1, source_target_pairs={{0,4},{2,6},{4,0},{6,2},{8,12},{10,14},{12,8},{14,10},{16,20},{18,... | collective-permute-start | bytes 208904 | tf_op jit(solution)/shard_map/ppermute | solution.py:389
  15.6 3.0 %copy-start = (f32[4,256]{1,0:T(4,128)S(1)}, f32[4,256]{1,0:T(4,128)}, u32[]{:S(2)}) copy-start(f32[4,256]{1,0:T(4,128)} %table_ref.1) | copy-start | bytes 12292
  15.6 3.0 %collective-permute-start.5 = (f32[8,8,128]{2,1,0:T(8,128)S(1)}, f32[8,8,128]{2,1,0:T(8,128)S(1)}, u32[]{:S(2)}, u32[]{:S(2)}) collective-permute-start(f32[8,8,128]{2,1,0:T(8,128)S(1)} %shard_map.40), channel_id=1, source_target_pairs={{0,2},{2,0},{4,6},{6,4},{8,10},{10,8},{12,14},{14,12},{16,18},{18,... | collective-permute-start | bytes 98312 | tf_op jit(solution)/shard_map/ppermute | solution.py:389
  15.6 4.6 %collective-permute-start.6 = (f32[2,8,128]{2,1,0:T(8,128)S(1)}, f32[2,8,128]{2,1,0:T(8,128)S(1)}, u32[]{:S(2)}, u32[]{:S(2)}) collective-permute-start(f32[2,8,128]{2,1,0:T(8,128)S(1)} %get-tuple-element.31), channel_id=1, source_target_pairs={{0,5},{1,4},{2,7},{3,6},{4,1},{5,0},{6,3},{7,2},{8,13},{9,12},{10,... | collective-permute-start | bytes 24584 | tf_op jit(solution)/shard_map/ppermute | solution.py:423
  18.1 3.7 %collective-permute-start.7 = (f32[2,8,128]{2,1,0:T(8,128)S(1)}, f32[2,8,128]{2,1,0:T(8,128)S(1)}, u32[]{:S(2)}, u32[]{:S(2)}) collective-permute-start(f32[2,8,128]{2,1,0:T(8,128)S(1)} %get-tuple-element.32), channel_id=1, source_target_pairs={{0,1},{1,0},{2,3},{3,2},{4,5},{5,4},{6,7},{7,6},{8,9},{9,8},{10,11... | collective-permute-start | bytes 24584 | tf_op jit(solution)/shard_map/ppermute | solution.py:422
